TPU v7x, 32 devices: a whole 2x2x4 slice. The times are simulated.
32 devices in a mesh: gx: 4 (over y, x), gy: 8 (over z, core).
Axes of the slice: x: 2, y: 2, z: 4, core: 2. Of those that a mesh axis runs over, the one named last changes fastest.
Arguments:
- velocity: float32 [3, 32, 128, 256], P(None, 'gx', 'gy'), may hold values from -6 to 6
- pressure: float32 [32, 128, 256], P('gx', 'gy'), may hold values from -4 to 4
- part_cell: int32 [4, 8, 8, 512], P('gx', 'gy'), may hold values from 0 to 32767
- part_count: int32 [4, 8, 8], P('gx', 'gy'), may hold values from 1 to 512, as said below
- grain_velocities: float32 [4, 8, 8, 3, 512], P('gx', 'gy'), may hold values from -6 to 6
- part_vol: float32 [4, 8, 8, 512], P('gx', 'gy'), may hold values from 0.05 to 0.3
Outputs:
- velocity_out: float32 [3, 32, 128, 256], P(None, 'gx', 'gy')
- pressure_out: float32 [32, 128, 256], P('gx', 'gy')
- drag: float32 [4, 8, 8, 3, 512], P('gx', 'gy')
Inputs may be any that keep to these rules, and one draw needn't show every extreme that they name: Every DEM owner (a, b) has at least one c with part_count[a, b, c] equal to 512.
All inputs are finite; a program needn't handle non-finite values.
Results may differ from a plain program's by a relative error of at most 0.00002.
Values sent between devices are 32-bit elements; how exact they have to be, the bound alone decides.
A program may use at most 128 MiB of HBM per device.

v0:
```python
import jax
import jax.numpy as jnp
from jax import lax
from jax.sharding import PartitionSpec as P

STEPS = 2
SWEEPS = 4
drag_coefficient = 2.0
time_step = 0.25
viscosity = 0.2
eps_floor = 0.4


def extended(block, sides, width):
    for axis, dim in sides:
        count = lax.axis_size(axis)
        forward = [(i, i + 1) for i in range(count - 1)]
        backward = [(target, source) for source, target in forward]
        low = lax.ppermute(
            lax.slice_in_dim(block, block.shape[dim] - width, None, axis=dim), axis, forward
        )
        high = lax.ppermute(lax.slice_in_dim(block, 0, width, axis=dim), axis, backward)
        block = jnp.concatenate([low, block, high], axis=dim)
    return block


def cell_faces(padded):
    return [
        padded[..., 2:, 1:-1, 1:-1],
        padded[..., :-2, 1:-1, 1:-1],
        padded[..., 1:-1, 2:, 1:-1],
        padded[..., 1:-1, :-2, 1:-1],
        padded[..., 1:-1, 1:-1, 2:],
        padded[..., 1:-1, 1:-1, :-2],
    ]


def padding_thickness(field):
    widths = [(0, 0)] * (field.ndim - 1) + [(1, 1)]
    return jnp.pad(field, widths)


def laplacian_operator(padded_velocity_field, flow_velocity, padded_voidage, porous_medium):
    near = cell_faces(padded_velocity_field)
    kernel_weights = cell_faces(padded_voidage)
    total = jnp.zeros_like(flow_velocity)
    for index in range(6):
        total = (
            total
            + 0.5
            * (porous_medium + kernel_weights[index])
            * (near[index] - flow_velocity)
            / porous_medium
        )
    return total


def divergence(flux_pad):
    near = cell_faces(flux_pad)
    return (
        0.5
        / time_step
        * (near[0][0] - near[1][0] + (near[2][1] - near[3][1]) + (near[4][2] - near[5][2]))
    )


def relaxation_terms(padded_pressure_field, padded_voidage):
    central_value = padded_voidage[1:-1, 1:-1, 1:-1]
    near = cell_faces(padded_pressure_field)
    kernel_weights = cell_faces(padded_voidage)
    numerator = jnp.zeros_like(central_value)
    denominator = jnp.zeros_like(central_value)
    for index in range(6):
        weight = 0.5 * (central_value + kernel_weights[index])
        numerator = numerator + weight * near[index]
        denominator = denominator + weight
    return (numerator, denominator)


def gradient(padded_pressure_field):
    near = cell_faces(padded_pressure_field)
    return jnp.stack(
        [0.5 * (near[0] - near[1]), 0.5 * (near[2] - near[3]), 0.5 * (near[4] - near[5])]
    )


def per_device(velocity, pressure, part_cell, part_count, grain_velocities, part_vol):
    rows_x, rows_y, depth = pressure.shape
    capacity = part_vol.shape[-1]
    grid_cells = rows_x * rows_y * depth
    slots = jnp.arange(capacity, dtype=jnp.int32)
    alive = slots[None, None, None, :] < part_count[..., None]
    grain_volume = jnp.where(alive, part_vol, jnp.float32(0.0))
    loads = jnp.concatenate([grain_velocities, grain_volume[..., None, :]], axis=3)
    got_cell = lax.all_to_all(part_cell, "gy", split_axis=2, concat_axis=2, tiled=True)
    got_load = lax.all_to_all(loads, "gy", split_axis=2, concat_axis=2, tiled=True)
    target_field = got_cell.reshape(-1)
    got_vol = got_load[..., 3, :]
    got_vel = got_load[..., :3, :]
    carried = jnp.moveaxis(got_vol[..., None, :] * got_vel, 3, 4).reshape(-1, 3)
    solid = jax.ops.segment_sum(got_vol.reshape(-1), target_field, num_segments=grid_cells).reshape(
        rows_x, rows_y, depth
    )
    mass_flux = jax.ops.segment_sum(carried, target_field, num_segments=grid_cells).T.reshape(
        3, rows_x, rows_y, depth
    )
    porous_medium = jnp.maximum(1.0 - solid, eps_floor)
    widened_field = extended(porous_medium, (("gx", 0), ("gy", 1)), 2)
    padded_voidage = padding_thickness(widened_field[1:-1, 1:-1])
    for step in range(STEPS):
        velocity_rotation = extended(velocity, (("gx", 1), ("gy", 2)), 1)
        spread_to_mesh = laplacian_operator(
            padding_thickness(velocity_rotation), velocity, padded_voidage, porous_medium
        )
        force = drag_coefficient * (mass_flux - solid * velocity) / porous_medium
        guess = velocity + time_step * (viscosity * spread_to_mesh + force)
        flux_cycle = extended(porous_medium * guess, (("gx", 1), ("gy", 2)), 1)
        source = divergence(padding_thickness(flux_cycle))
        for sweep in range(SWEEPS):
            pressure_rotation = extended(pressure, (("gx", 0), ("gy", 1)), 1)
            numerator, denominator = relaxation_terms(
                padding_thickness(pressure_rotation), padded_voidage
            )
            pressure = (numerator - source) / denominator
        slope_cycle = extended(pressure, (("gx", 0), ("gy", 1)), 1)
        velocity = guess - time_step * gradient(padding_thickness(slope_cycle))
    flat_vel = velocity.reshape(3, grid_cells)
    flattened_voids = porous_medium.reshape(grid_cells)
    slot_shape_factors = got_vol.shape
    cell_flow_speed = jnp.moveaxis(
        flat_vel[:, target_field].reshape((3,) + slot_shape_factors), 0, 3
    )
    cell_void_fraction = flattened_voids[target_field].reshape(slot_shape_factors)
    coupled_state = jnp.concatenate([cell_flow_speed, cell_void_fraction[..., None, :]], axis=3)
    back = lax.all_to_all(coupled_state, "gy", split_axis=2, concat_axis=2, tiled=True)
    drag = (
        grain_volume[..., None, :]
        * drag_coefficient
        * (back[..., :3, :] - grain_velocities)
        / back[..., 3:4, :]
    )
    return (velocity, pressure, drag)


def solution(mesh):
    placed = (
        P(None, "gx", "gy", None),
        P("gx", "gy", None),
        P("gx", "gy", None, None),
        P("gx", "gy", None),
        P("gx", "gy", None, None, None),
        P("gx", "gy", None, None),
    )
    return jax.shard_map(
        per_device,
        mesh=mesh,
        in_specs=placed,
        out_specs=(P(None, "gx", "gy", None), P("gx", "gy", None), P("gx", "gy", None, None, None)),
        check_vma=False,
    )
```

profile of v0, /device:TPU:4, one launch (start us, length us, event | category | flops | bytes accessed | tf_op | source)
XLA Modules:
  0.0 359.1 jit_solution(8799463692055073704)
XLA Ops:
  3.6 4.9 %all-to-all-start.1 = ((f32[1,1,8,4,512]{4,3,1,0,2:T(4,128)}), f32[1,1,8,4,512]{4,3,1,0,2:T(4,128)S(1)}, u32[]{:S(2)}, u32[]{:S(2)}) async-start(f32[1,1,8,4,512]{4,3,1,0,2:T(4,128)} %pad_maximum_fusion.104), calls=%async_computation.1 | async-start | bytes 131072 | tf_op jit(solution)/shard_map/all_to_all | solution.py:96
  9.2 3.4 collective-permute-start.9
  15.4 4.8 %collective-permute-start.1 = (f32[3,1,16,256]{3,2,1,0:T(8,128)S(1)}, f32[3,1,16,256]{3,2,1,0:T(8,128)S(1)}, u32[]{:S(2)}, u32[]{:S(2)}) collective-permute-start(f32[3,1,16,256]{3,2,1,0:T(8,128)S(1)} %get-tuple-element.35), channel_id=1, source_target_pairs={{8,0},{16,8},{24,16},{9,1},{17,9},{25,17},{10,2},{18,10},{26,18},{... | collective-permute-start | bytes 147464 | tf_op jit(solution)/shard_map/ppermute | solution.py:22
  25.9 5.1 %all-to-all-start = ((s32[1,1,8,512]{3,1,0,2:T(1,128)}), s32[1,1,8,512]{3,1,0,2:T(1,128)S(1)}, u32[]{:S(2)}, u32[]{:S(2)}) async-start(s32[1,1,8,512]{3,1,0,2:T(1,128)} %copy.25), calls=%async_computation | async-start | bytes 32768 | tf_op jit(solution)/shard_map/all_to_all | solution.py:95
  32.4 3.0 collective-permute-start.7
  36.7 21.9 %scatter_custom_fusion = f32[32768]{0:T(1024)S(1)} fusion(s32[4096]{0:T(1024)S(1)} %bitcast.52, f32[4096]{0:T(1024)S(1)} %bitcast.56, f32[]{:T(128)} %constant.10.clone.1), kind=kCustom, calls=%fused_computation.368 | custom fusion | flops 4096 | bytes 131076 | tf_op jit(solution)/shard_map/scatter-add | solution.py:101
  59.4 3.3 collective-permute-start
  65.9 3.5 collective-permute-done.2
  70.8 3.0 collective-permute-start.6
  75.8 29.5 %scatter_custom_fusion.1 = f32[32768,3]{1,0:T(8,128)} fusion(s32[4096]{0:T(1024)S(1)} %bitcast.53, f32[4096,3]{1,0:T(8,128)} %copy.29, f32[]{:T(128)} %constant.10.clone.1), kind=kCustom, calls=%fused_computation.4 | custom fusion | flops 12288 | bytes 393728 | tf_op jit(solution)/shard_map/scatter-add | solution.py:104
  105.4 10.0 %copy.30 = f32[3,8,16,256]{3,2,1,0:T(8,128)S(1)} copy(f32[3,8,16,256]{0,3,2,1:T(8,128)} %bitcast.45) | data formatting | bytes 786432 | tf_op jit(solution)/shard_map/reshape | solution.py:104
  120.3 3.9 %collective-permute-start.13 = (f32[3,1,16,256]{3,2,1,0:T(8,128)S(1)}, f32[3,1,16,256]{3,2,1,0:T(8,128)S(1)}, u32[]{:S(2)}, u32[]{:S(2)}) collective-permute-start(f32[3,1,16,256]{3,2,1,0:T(8,128)S(1)} %get-tuple-element.33), channel_id=1, source_target_pairs={{0,8},{8,16},{16,24},{1,9},{9,17},{17,25},{2,10},{10,18},{18,26},{... | collective-permute-start | bytes 147464 | tf_op jit(solution)/shard_map/ppermute | solution.py:19
  125.6 3.0 collective-permute-start.11
  130.0 4.0 %collective-permute-start.15 = (f32[3,10,1,256]{3,2,1,0:T(1,128)S(1)}, f32[3,10,1,256]{3,2,1,0:T(1,128)S(1)}, u32[]{:S(2)}, u32[]{:S(2)}) collective-permute-start(f32[3,10,1,256]{3,2,1,0:T(1,128)S(1)} %get-tuple-element.25), channel_id=1, source_target_pairs={{0,1},{1,2},{2,3},{3,4},{4,5},{5,6},{6,7},{8,9},{9,10},{10,11},{11... | collective-permute-start | bytes 92168 | tf_op jit(solution)/shard_map/ppermute | solution.py:19
  135.8 3.1 collective-permute-start.16
  139.0 2.7 collective-permute-start.17
  141.7 3.8 %collective-permute-done.17 = f32[1,16,256]{2,1,0:T(8,128)S(1)} collective-permute-done((f32[1,16,256]{2,1,0:T(8,128)S(1)}, f32[1,16,256]{2,1,0:T(8,128)S(1)}, u32[]{:S(2)}, u32[]{:S(2)}) %collective-permute-start.17) | collective-permute-done | bytes 16416 | tf_op jit(solution)/shard_map/ppermute | solution.py:19
  146.8 3.0 collective-permute-start.19
  153.0 3.9 %collective-permute-start.21 = (f32[1,16,256]{2,1,0:T(8,128)S(1)}, f32[1,16,256]{2,1,0:T(8,128)S(1)}, u32[]{:S(2)}, u32[]{:S(2)}) collective-permute-start(f32[1,16,256]{2,1,0:T(8,128)S(1)} %get-tuple-element.77), channel_id=1, source_target_pairs={{0,8},{8,16},{16,24},{1,9},{9,17},{17,25},{2,10},{10,18},{18,26},{... | collective-permute-start | bytes 49160 | tf_op jit(solution)/shard_map/ppermute | solution.py:19
  160.9 5.2 %collective-permute-start.23 = (f32[10,1,256]{2,1,0:T(1,128)S(1)}, f32[10,1,256]{2,1,0:T(1,128)S(1)}, u32[]{:S(2)}, u32[]{:S(2)}) collective-permute-start(f32[10,1,256]{2,1,0:T(1,128)S(1)} %get-tuple-element.57), channel_id=1, source_target_pairs={{0,1},{1,2},{2,3},{3,4},{4,5},{5,6},{6,7},{8,9},{9,10},{10,11},{11... | collective-permute-start | bytes 30728 | tf_op jit(solution)/shard_map/ppermute | solution.py:19
  169.1 3.9 %collective-permute-start.25 = (f32[1,16,256]{2,1,0:T(8,128)S(1)}, f32[1,16,256]{2,1,0:T(8,128)S(1)}, u32[]{:S(2)}, u32[]{:S(2)}) collective-permute-start(f32[1,16,256]{2,1,0:T(8,128)S(1)} %get-tuple-element.75), channel_id=1, source_target_pairs={{0,8},{8,16},{16,24},{1,9},{9,17},{17,25},{2,10},{10,18},{18,26},{... | collective-permute-start | bytes 49160 | tf_op jit(solution)/shard_map/ppermute | solution.py:19
  173.0 2.6 collective-permute-done.25
  177.0 4.8 %collective-permute-start.27 = (f32[10,1,256]{2,1,0:T(1,128)S(1)}, f32[10,1,256]{2,1,0:T(1,128)S(1)}, u32[]{:S(2)}, u32[]{:S(2)}) collective-permute-start(f32[10,1,256]{2,1,0:T(1,128)S(1)} %get-tuple-element.55), channel_id=1, source_target_pairs={{0,1},{1,2},{2,3},{3,4},{4,5},{5,6},{6,7},{8,9},{9,10},{10,11},{11... | collective-permute-start | bytes 30728 | tf_op jit(solution)/shard_map/ppermute | solution.py:19
  184.9 3.9 %collective-permute-start.29 = (f32[1,16,256]{2,1,0:T(8,128)S(1)}, f32[1,16,256]{2,1,0:T(8,128)S(1)}, u32[]{:S(2)}, u32[]{:S(2)}) collective-permute-start(f32[1,16,256]{2,1,0:T(8,128)S(1)} %get-tuple-element.73), channel_id=1, source_target_pairs={{0,8},{8,16},{16,24},{1,9},{9,17},{17,25},{2,10},{10,18},{18,26},{... | collective-permute-start | bytes 49160 | tf_op jit(solution)/shard_map/ppermute | solution.py:19
  188.8 2.6 collective-permute-done.29
  192.8 4.8 %collective-permute-start.31 = (f32[10,1,256]{2,1,0:T(1,128)S(1)}, f32[10,1,256]{2,1,0:T(1,128)S(1)}, u32[]{:S(2)}, u32[]{:S(2)}) collective-permute-start(f32[10,1,256]{2,1,0:T(1,128)S(1)} %get-tuple-element.53), channel_id=1, source_target_pairs={{0,1},{1,2},{2,3},{3,4},{4,5},{5,6},{6,7},{8,9},{9,10},{10,11},{11... | collective-permute-start | bytes 30728 | tf_op jit(solution)/shard_map/ppermute | solution.py:19
  200.8 3.9 %collective-permute-start.33 = (f32[3,1,16,256]{3,2,1,0:T(8,128)S(1)}, f32[3,1,16,256]{3,2,1,0:T(8,128)S(1)}, u32[]{:S(2)}, u32[]{:S(2)}) collective-permute-start(f32[3,1,16,256]{3,2,1,0:T(8,128)S(1)} %get-tuple-element.31), channel_id=1, source_target_pairs={{0,8},{8,16},{16,24},{1,9},{9,17},{17,25},{2,10},{10,18},{18,26},{... | collective-permute-start | bytes 147464 | tf_op jit(solution)/shard_map/ppermute | solution.py:19
  204.9 2.8 collective-permute-done.33
  209.1 4.8 %collective-permute-start.35 = (f32[3,10,1,256]{3,2,1,0:T(1,128)S(1)}, f32[3,10,1,256]{3,2,1,0:T(1,128)S(1)}, u32[]{:S(2)}, u32[]{:S(2)}) collective-permute-start(f32[3,10,1,256]{3,2,1,0:T(1,128)S(1)} %get-tuple-element.23), channel_id=1, source_target_pairs={{0,1},{1,2},{2,3},{3,4},{4,5},{5,6},{6,7},{8,9},{9,10},{10,11},{11... | collective-permute-start | bytes 92168 | tf_op jit(solution)/shard_map/ppermute | solution.py:19
  217.8 3.9 %collective-permute-start.37 = (f32[3,1,16,256]{3,2,1,0:T(8,128)S(1)}, f32[3,1,16,256]{3,2,1,0:T(8,128)S(1)}, u32[]{:S(2)}, u32[]{:S(2)}) collective-permute-start(f32[3,1,16,256]{3,2,1,0:T(8,128)S(1)} %get-tuple-element.29), channel_id=1, source_target_pairs={{0,8},{8,16},{16,24},{1,9},{9,17},{17,25},{2,10},{10,18},{18,26},{... | collective-permute-start | bytes 147464 | tf_op jit(solution)/shard_map/ppermute | solution.py:19
  221.9 2.8 collective-permute-done.37
  226.1 5.0 %collective-permute-start.39 = (f32[3,10,1,256]{3,2,1,0:T(1,128)S(1)}, f32[3,10,1,256]{3,2,1,0:T(1,128)S(1)}, u32[]{:S(2)}, u32[]{:S(2)}) collective-permute-start(f32[3,10,1,256]{3,2,1,0:T(1,128)S(1)} %get-tuple-element.21), channel_id=1, source_target_pairs={{0,1},{1,2},{2,3},{3,4},{4,5},{5,6},{6,7},{8,9},{9,10},{10,11},{11... | collective-permute-start | bytes 92168 | tf_op jit(solution)/shard_map/ppermute | solution.py:19
  234.7 3.9 %collective-permute-start.41 = (f32[1,16,256]{2,1,0:T(8,128)S(1)}, f32[1,16,256]{2,1,0:T(8,128)S(1)}, u32[]{:S(2)}, u32[]{:S(2)}) collective-permute-start(f32[1,16,256]{2,1,0:T(8,128)S(1)} %get-tuple-element.71), channel_id=1, source_target_pairs={{0,8},{8,16},{16,24},{1,9},{9,17},{17,25},{2,10},{10,18},{18,26},{... | collective-permute-start | bytes 49160 | tf_op jit(solution)/shard_map/ppermute | solution.py:19
  242.6 5.0 %collective-permute-start.43 = (f32[10,1,256]{2,1,0:T(1,128)S(1)}, f32[10,1,256]{2,1,0:T(1,128)S(1)}, u32[]{:S(2)}, u32[]{:S(2)}) collective-permute-start(f32[10,1,256]{2,1,0:T(1,128)S(1)} %get-tuple-element.49), channel_id=1, source_target_pairs={{0,1},{1,2},{2,3},{3,4},{4,5},{5,6},{6,7},{8,9},{9,10},{10,11},{11... | collective-permute-start | bytes 30728 | tf_op jit(solution)/shard_map/ppermute | solution.py:19
  250.7 3.9 %collective-permute-start.45 = (f32[1,16,256]{2,1,0:T(8,128)S(1)}, f32[1,16,256]{2,1,0:T(8,128)S(1)}, u32[]{:S(2)}, u32[]{:S(2)}) collective-permute-start(f32[1,16,256]{2,1,0:T(8,128)S(1)} %get-tuple-element.69), channel_id=1, source_target_pairs={{0,8},{8,16},{16,24},{1,9},{9,17},{17,25},{2,10},{10,18},{18,26},{... | collective-permute-start | bytes 49160 | tf_op jit(solution)/shard_map/ppermute | solution.py:19
  254.7 2.6 collective-permute-done.45
  258.6 4.8 %collective-permute-start.47 = (f32[10,1,256]{2,1,0:T(1,128)S(1)}, f32[10,1,256]{2,1,0:T(1,128)S(1)}, u32[]{:S(2)}, u32[]{:S(2)}) collective-permute-start(f32[10,1,256]{2,1,0:T(1,128)S(1)} %get-tuple-element.47), channel_id=1, source_target_pairs={{0,1},{1,2},{2,3},{3,4},{4,5},{5,6},{6,7},{8,9},{9,10},{10,11},{11... | collective-permute-start | bytes 30728 | tf_op jit(solution)/shard_map/ppermute | solution.py:19
  266.6 3.9 %collective-permute-start.49 = (f32[1,16,256]{2,1,0:T(8,128)S(1)}, f32[1,16,256]{2,1,0:T(8,128)S(1)}, u32[]{:S(2)}, u32[]{:S(2)}) collective-permute-start(f32[1,16,256]{2,1,0:T(8,128)S(1)} %get-tuple-element.67), channel_id=1, source_target_pairs={{0,8},{8,16},{16,24},{1,9},{9,17},{17,25},{2,10},{10,18},{18,26},{... | collective-permute-start | bytes 49160 | tf_op jit(solution)/shard_map/ppermute | solution.py:19
  270.5 2.6 collective-permute-done.49
  274.5 4.8 %collective-permute-start.51 = (f32[10,1,256]{2,1,0:T(1,128)S(1)}, f32[10,1,256]{2,1,0:T(1,128)S(1)}, u32[]{:S(2)}, u32[]{:S(2)}) collective-permute-start(f32[10,1,256]{2,1,0:T(1,128)S(1)} %get-tuple-element.45), channel_id=1, source_target_pairs={{0,1},{1,2},{2,3},{3,4},{4,5},{5,6},{6,7},{8,9},{9,10},{10,11},{11... | collective-permute-start | bytes 30728 | tf_op jit(solution)/shard_map/ppermute | solution.py:19
  282.4 3.9 %collective-permute-start.53 = (f32[1,16,256]{2,1,0:T(8,128)S(1)}, f32[1,16,256]{2,1,0:T(8,128)S(1)}, u32[]{:S(2)}, u32[]{:S(2)}) collective-permute-start(f32[1,16,256]{2,1,0:T(8,128)S(1)} %get-tuple-element.65), channel_id=1, source_target_pairs={{0,8},{8,16},{16,24},{1,9},{9,17},{17,25},{2,10},{10,18},{18,26},{... | collective-permute-start | bytes 49160 | tf_op jit(solution)/shard_map/ppermute | solution.py:19
  286.4 2.6 collective-permute-done.53
  290.3 4.8 %collective-permute-start.55 = (f32[10,1,256]{2,1,0:T(1,128)S(1)}, f32[10,1,256]{2,1,0:T(1,128)S(1)}, u32[]{:S(2)}, u32[]{:S(2)}) collective-permute-start(f32[10,1,256]{2,1,0:T(1,128)S(1)} %get-tuple-element.43), channel_id=1, source_target_pairs={{0,1},{1,2},{2,3},{3,4},{4,5},{5,6},{6,7},{8,9},{9,10},{10,11},{11... | collective-permute-start | bytes 30728 | tf_op jit(solution)/shard_map/ppermute | solution.py:19
  295.1 23.0 %gather_fusion.1 = f32[4096]{0:T(1024)S(1)} fusion(f32[32768]{0:T(1024)S(1)} %subtract_maximum_fusion, s32[4096]{0:T(1024)S(1)} %broadcast_clamp_fusion), kind=kCustom, calls=%fused_computation.1 | custom fusion | bytes 49152 | tf_op jit(solution)/shard_map/gather | solution.py:133
  318.7 8.7 %copy.32 = f32[3,8,16,256]{0,3,2,1:T(8,128)} copy(f32[3,8,16,256]{3,2,1,0:T(8,128)S(1)} %fusion.54) | data formatting | bytes 786432 | tf_op jit(solution)/shard_map/sub | solution.py:126
  327.4 16.5 %gather_fusion = f32[4096,3]{1,0:T(8,128)S(1)} fusion(f32[3,32768]{0,1:T(8,128)} %bitcast.46, s32[4096]{0:T(1024)S(1)} %broadcast_clamp_fusion), kind=kCustom, calls=%fused_computation | custom fusion | bytes 114688 | tf_op jit(solution)/shard_map/gather | solution.py:131
  345.3 7.2 %all-to-all-start.2 = ((f32[1,1,8,4,512]{4,3,1,0,2:T(4,128)}), f32[1,1,8,4,512]{4,3,1,0,2:T(4,128)S(1)}, u32[]{:S(2)}, u32[]{:S(2)}) async-start(f32[1,1,8,4,512]{4,3,1,0,2:T(4,128)} %pad_maximum_fusion.105), calls=%async_computation.2 | async-start | bytes 131072 | tf_op jit(solution)/shard_map/all_to_all | solution.py:135
  352.5 5.9 %all-to-all-done.2 = f32[1,1,8,4,512]{4,3,1,0,2:T(4,128)S(1)} async-done(((f32[1,1,8,4,512]{4,3,1,0,2:T(4,128)}), f32[1,1,8,4,512]{4,3,1,0,2:T(4,128)S(1)}, u32[]{:S(2)}, u32[]{:S(2)}) %all-to-all-start.2) | async-done | bytes 65568 | tf_op jit(solution)/shard_map/all_to_all | solution.py:135
  (209 shorter events, 81.6 us)
Async XLA Ops:
  3.6 22.3 %all-to-all-start.1 = ((f32[1,1,8,4,512]{4,3,1,0,2:T(4,128)}), f32[1,1,8,4,512]{4,3,1,0,2:T(4,128)S(1)}, u32[]{:S(2)}, u32[]{:S(2)}) async-start(f32[1,1,8,4,512]{4,3,1,0,2:T(4,128)} %pad_maximum_fusion.104), calls=%async_computation.1 | async-start | bytes 131072 | tf_op jit(solution)/shard_map/all_to_all | solution.py:96
  9.2 14.8 %collective-permute-start.9 = (f32[1,16,256]{2,1,0:T(8,128)S(1)}, f32[1,16,256]{2,1,0:T(8,128)S(1)}, u32[]{:S(2)}, u32[]{:S(2)}) collective-permute-start(f32[1,16,256]{2,1,0:T(8,128)S(1)} %get-tuple-element.82), channel_id=1, source_target_pairs={{0,8},{8,16},{16,24},{1,9},{9,17},{17,25},{2,10},{10,18},{18,26},{... | collective-permute-start | bytes 49160 | tf_op jit(solution)/shard_map/ppermute | solution.py:19
  13.4 12.4 %collective-permute-start.3 = (f32[3,1,16,256]{3,2,1,0:T(8,128)S(1)}, f32[3,1,16,256]{3,2,1,0:T(8,128)S(1)}, u32[]{:S(2)}, u32[]{:S(2)}) collective-permute-start(f32[3,1,16,256]{3,2,1,0:T(8,128)S(1)} %get-tuple-element.36), channel_id=1, source_target_pairs={{0,8},{8,16},{16,24},{1,9},{9,17},{17,25},{2,10},{10,18},{18,26},{... | collective-permute-start | bytes 147464 | tf_op jit(solution)/shard_map/ppermute | solution.py:19
  15.4 10.5 %collective-permute-start.1 = (f32[3,1,16,256]{3,2,1,0:T(8,128)S(1)}, f32[3,1,16,256]{3,2,1,0:T(8,128)S(1)}, u32[]{:S(2)}, u32[]{:S(2)}) collective-permute-start(f32[3,1,16,256]{3,2,1,0:T(8,128)S(1)} %get-tuple-element.35), channel_id=1, source_target_pairs={{8,0},{16,8},{24,16},{9,1},{17,9},{25,17},{10,2},{18,10},{26,18},{... | collective-permute-start | bytes 147464 | tf_op jit(solution)/shard_map/ppermute | solution.py:22
  25.9 10.8 %all-to-all-start = ((s32[1,1,8,512]{3,1,0,2:T(1,128)}), s32[1,1,8,512]{3,1,0,2:T(1,128)S(1)}, u32[]{:S(2)}, u32[]{:S(2)}) async-start(s32[1,1,8,512]{3,1,0,2:T(1,128)} %copy.25), calls=%async_computation | async-start | bytes 32768 | tf_op jit(solution)/shard_map/all_to_all | solution.py:95
  31.1 34.2 %collective-permute-start.5 = (f32[3,10,1,256]{3,2,1,0:T(1,128)S(1)}, f32[3,10,1,256]{3,2,1,0:T(1,128)S(1)}, u32[]{:S(2)}, u32[]{:S(2)}) collective-permute-start(f32[3,10,1,256]{3,2,1,0:T(1,128)S(1)} %get-tuple-element.28), channel_id=1, source_target_pairs={{1,0},{2,1},{3,2},{4,3},{5,4},{6,5},{7,6},{9,8},{10,9},{11,10},{12... | collective-permute-start | bytes 92168 | tf_op jit(solution)/shard_map/ppermute | solution.py:22
  32.4 32.9 %collective-permute-start.7 = (f32[3,10,1,256]{3,2,1,0:T(1,128)S(1)}, f32[3,10,1,256]{3,2,1,0:T(1,128)S(1)}, u32[]{:S(2)}, u32[]{:S(2)}) collective-permute-start(f32[3,10,1,256]{3,2,1,0:T(1,128)S(1)} %get-tuple-element.27), channel_id=1, source_target_pairs={{0,1},{1,2},{2,3},{3,4},{4,5},{5,6},{6,7},{8,9},{9,10},{10,11},{11... | collective-permute-start | bytes 92168 | tf_op jit(solution)/shard_map/ppermute | solution.py:19
  59.4 6.5 %collective-permute-start = (f32[2,16,256]{2,1,0:T(8,128)S(1)}, f32[2,16,256]{2,1,0:T(8,128)S(1)}, u32[]{:S(2)}, u32[]{:S(2)}) collective-permute-start(f32[2,16,256]{2,1,0:T(8,128)S(1)} %get-tuple-element.84), channel_id=1, source_target_pairs={{8,0},{16,8},{24,16},{9,1},{17,9},{25,17},{10,2},{18,10},{26,18},{... | collective-permute-start | bytes 98312 | tf_op jit(solution)/shard_map/ppermute | solution.py:22
  62.8 6.7 %collective-permute-start.2 = (f32[2,16,256]{2,1,0:T(8,128)S(1)}, f32[2,16,256]{2,1,0:T(8,128)S(1)}, u32[]{:S(2)}, u32[]{:S(2)}) collective-permute-start(f32[2,16,256]{2,1,0:T(8,128)S(1)} %get-tuple-element.83), channel_id=1, source_target_pairs={{0,8},{8,16},{16,24},{1,9},{9,17},{17,25},{2,10},{10,18},{18,26},{... | collective-permute-start | bytes 98312 | tf_op jit(solution)/shard_map/ppermute | solution.py:19
  69.5 45.9 %collective-permute-start.4 = (f32[12,2,256]{2,1,0:T(2,128)S(1)}, f32[12,2,256]{2,1,0:T(2,128)S(1)}, u32[]{:S(2)}, u32[]{:S(2)}) collective-permute-start(f32[12,2,256]{2,1,0:T(2,128)S(1)} %get-tuple-element.40), channel_id=1, source_target_pairs={{1,0},{2,1},{3,2},{4,3},{5,4},{6,5},{7,6},{9,8},{10,9},{11,10},{12... | collective-permute-start | bytes 73736 | tf_op jit(solution)/shard_map/ppermute | solution.py:22
  70.8 44.6 %collective-permute-start.6 = (f32[12,2,256]{2,1,0:T(2,128)S(1)}, f32[12,2,256]{2,1,0:T(2,128)S(1)}, u32[]{:S(2)}, u32[]{:S(2)}) collective-permute-start(f32[12,2,256]{2,1,0:T(2,128)S(1)} %get-tuple-element.39), channel_id=1, source_target_pairs={{0,1},{1,2},{2,3},{3,4},{4,5},{5,6},{6,7},{8,9},{9,10},{10,11},{11... | collective-permute-start | bytes 73736 | tf_op jit(solution)/shard_map/ppermute | solution.py:19
  118.4 10.2 %collective-permute-start.12 = (f32[3,1,16,256]{3,2,1,0:T(8,128)S(1)}, f32[3,1,16,256]{3,2,1,0:T(8,128)S(1)}, u32[]{:S(2)}, u32[]{:S(2)}) collective-permute-start(f32[3,1,16,256]{3,2,1,0:T(8,128)S(1)} %get-tuple-element.34), channel_id=1, source_target_pairs={{8,0},{16,8},{24,16},{9,1},{17,9},{25,17},{10,2},{18,10},{26,18},{... | collective-permute-start | bytes 147464 | tf_op jit(solution)/shard_map/ppermute | solution.py:22
  120.3 8.3 %collective-permute-start.13 = (f32[3,1,16,256]{3,2,1,0:T(8,128)S(1)}, f32[3,1,16,256]{3,2,1,0:T(8,128)S(1)}, u32[]{:S(2)}, u32[]{:S(2)}) collective-permute-start(f32[3,1,16,256]{3,2,1,0:T(8,128)S(1)} %get-tuple-element.33), channel_id=1, source_target_pairs={{0,8},{8,16},{16,24},{1,9},{9,17},{17,25},{2,10},{10,18},{18,26},{... | collective-permute-start | bytes 147464 | tf_op jit(solution)/shard_map/ppermute | solution.py:19
  124.3 9.8 %collective-permute-start.10 = (f32[10,1,256]{2,1,0:T(1,128)S(1)}, f32[10,1,256]{2,1,0:T(1,128)S(1)}, u32[]{:S(2)}, u32[]{:S(2)}) collective-permute-start(f32[10,1,256]{2,1,0:T(1,128)S(1)} %get-tuple-element.62), channel_id=1, source_target_pairs={{1,0},{2,1},{3,2},{4,3},{5,4},{6,5},{7,6},{9,8},{10,9},{11,10},{12... | collective-permute-start | bytes 30728 | tf_op jit(solution)/shard_map/ppermute | solution.py:22
  125.6 8.5 %collective-permute-start.11 = (f32[10,1,256]{2,1,0:T(1,128)S(1)}, f32[10,1,256]{2,1,0:T(1,128)S(1)}, u32[]{:S(2)}, u32[]{:S(2)}) collective-permute-start(f32[10,1,256]{2,1,0:T(1,128)S(1)} %get-tuple-element.61), channel_id=1, source_target_pairs={{0,1},{1,2},{2,3},{3,4},{4,5},{5,6},{6,7},{8,9},{9,10},{10,11},{11... | collective-permute-start | bytes 30728 | tf_op jit(solution)/shard_map/ppermute | solution.py:19
  135.8 5.9 %collective-permute-start.16 = (f32[1,16,256]{2,1,0:T(8,128)S(1)}, f32[1,16,256]{2,1,0:T(8,128)S(1)}, u32[]{:S(2)}, u32[]{:S(2)}) collective-permute-start(f32[1,16,256]{2,1,0:T(8,128)S(1)} %get-tuple-element.80), channel_id=1, source_target_pairs={{8,0},{16,8},{24,16},{9,1},{17,9},{25,17},{10,2},{18,10},{26,18},{... | collective-permute-start | bytes 49160 | tf_op jit(solution)/shard_map/ppermute | solution.py:22
  139.0 6.5 %collective-permute-start.17 = (f32[1,16,256]{2,1,0:T(8,128)S(1)}, f32[1,16,256]{2,1,0:T(8,128)S(1)}, u32[]{:S(2)}, u32[]{:S(2)}) collective-permute-start(f32[1,16,256]{2,1,0:T(8,128)S(1)} %get-tuple-element.79), channel_id=1, source_target_pairs={{0,8},{8,16},{16,24},{1,9},{9,17},{17,25},{2,10},{10,18},{18,26},{... | collective-permute-start | bytes 49160 | tf_op jit(solution)/shard_map/ppermute | solution.py:19
  151.1 5.9 %collective-permute-start.20 = (f32[1,16,256]{2,1,0:T(8,128)S(1)}, f32[1,16,256]{2,1,0:T(8,128)S(1)}, u32[]{:S(2)}, u32[]{:S(2)}) collective-permute-start(f32[1,16,256]{2,1,0:T(8,128)S(1)} %get-tuple-element.78), channel_id=1, source_target_pairs={{8,0},{16,8},{24,16},{9,1},{17,9},{25,17},{10,2},{18,10},{26,18},{... | collective-permute-start | bytes 49160 | tf_op jit(solution)/shard_map/ppermute | solution.py:22
  153.0 6.5 %collective-permute-start.21 = (f32[1,16,256]{2,1,0:T(8,128)S(1)}, f32[1,16,256]{2,1,0:T(8,128)S(1)}, u32[]{:S(2)}, u32[]{:S(2)}) collective-permute-start(f32[1,16,256]{2,1,0:T(8,128)S(1)} %get-tuple-element.77), channel_id=1, source_target_pairs={{0,8},{8,16},{16,24},{1,9},{9,17},{17,25},{2,10},{10,18},{18,26},{... | collective-permute-start | bytes 49160 | tf_op jit(solution)/shard_map/ppermute | solution.py:19
  159.6 6.6 %collective-permute-start.22 = (f32[10,1,256]{2,1,0:T(1,128)S(1)}, f32[10,1,256]{2,1,0:T(1,128)S(1)}, u32[]{:S(2)}, u32[]{:S(2)}) collective-permute-start(f32[10,1,256]{2,1,0:T(1,128)S(1)} %get-tuple-element.58), channel_id=1, source_target_pairs={{1,0},{2,1},{3,2},{4,3},{5,4},{6,5},{7,6},{9,8},{10,9},{11,10},{12... | collective-permute-start | bytes 30728 | tf_op jit(solution)/shard_map/ppermute | solution.py:22
  160.9 5.9 %collective-permute-start.23 = (f32[10,1,256]{2,1,0:T(1,128)S(1)}, f32[10,1,256]{2,1,0:T(1,128)S(1)}, u32[]{:S(2)}, u32[]{:S(2)}) collective-permute-start(f32[10,1,256]{2,1,0:T(1,128)S(1)} %get-tuple-element.57), channel_id=1, source_target_pairs={{0,1},{1,2},{2,3},{3,4},{4,5},{5,6},{6,7},{8,9},{9,10},{10,11},{11... | collective-permute-start | bytes 30728 | tf_op jit(solution)/shard_map/ppermute | solution.py:19
  167.2 5.9 %collective-permute-start.24 = (f32[1,16,256]{2,1,0:T(8,128)S(1)}, f32[1,16,256]{2,1,0:T(8,128)S(1)}, u32[]{:S(2)}, u32[]{:S(2)}) collective-permute-start(f32[1,16,256]{2,1,0:T(8,128)S(1)} %get-tuple-element.76), channel_id=1, source_target_pairs={{8,0},{16,8},{24,16},{9,1},{17,9},{25,17},{10,2},{18,10},{26,18},{... | collective-permute-start | bytes 49160 | tf_op jit(solution)/shard_map/ppermute | solution.py:22
  169.1 6.5 %collective-permute-start.25 = (f32[1,16,256]{2,1,0:T(8,128)S(1)}, f32[1,16,256]{2,1,0:T(8,128)S(1)}, u32[]{:S(2)}, u32[]{:S(2)}) collective-permute-start(f32[1,16,256]{2,1,0:T(8,128)S(1)} %get-tuple-element.75), channel_id=1, source_target_pairs={{0,8},{8,16},{16,24},{1,9},{9,17},{17,25},{2,10},{10,18},{18,26},{... | collective-permute-start | bytes 49160 | tf_op jit(solution)/shard_map/ppermute | solution.py:19
  175.7 6.1 %collective-permute-start.26 = (f32[10,1,256]{2,1,0:T(1,128)S(1)}, f32[10,1,256]{2,1,0:T(1,128)S(1)}, u32[]{:S(2)}, u32[]{:S(2)}) collective-permute-start(f32[10,1,256]{2,1,0:T(1,128)S(1)} %get-tuple-element.56), channel_id=1, source_target_pairs={{1,0},{2,1},{3,2},{4,3},{5,4},{6,5},{7,6},{9,8},{10,9},{11,10},{12... | collective-permute-start | bytes 30728 | tf_op jit(solution)/shard_map/ppermute | solution.py:22
  183.0 5.9 %collective-permute-start.28 = (f32[1,16,256]{2,1,0:T(8,128)S(1)}, f32[1,16,256]{2,1,0:T(8,128)S(1)}, u32[]{:S(2)}, u32[]{:S(2)}) collective-permute-start(f32[1,16,256]{2,1,0:T(8,128)S(1)} %get-tuple-element.74), channel_id=1, source_target_pairs={{8,0},{16,8},{24,16},{9,1},{17,9},{25,17},{10,2},{18,10},{26,18},{... | collective-permute-start | bytes 49160 | tf_op jit(solution)/shard_map/ppermute | solution.py:22
  184.9 6.5 %collective-permute-start.29 = (f32[1,16,256]{2,1,0:T(8,128)S(1)}, f32[1,16,256]{2,1,0:T(8,128)S(1)}, u32[]{:S(2)}, u32[]{:S(2)}) collective-permute-start(f32[1,16,256]{2,1,0:T(8,128)S(1)} %get-tuple-element.73), channel_id=1, source_target_pairs={{0,8},{8,16},{16,24},{1,9},{9,17},{17,25},{2,10},{10,18},{18,26},{... | collective-permute-start | bytes 49160 | tf_op jit(solution)/shard_map/ppermute | solution.py:19
  191.5 6.1 %collective-permute-start.30 = (f32[10,1,256]{2,1,0:T(1,128)S(1)}, f32[10,1,256]{2,1,0:T(1,128)S(1)}, u32[]{:S(2)}, u32[]{:S(2)}) collective-permute-start(f32[10,1,256]{2,1,0:T(1,128)S(1)} %get-tuple-element.54), channel_id=1, source_target_pairs={{1,0},{2,1},{3,2},{4,3},{5,4},{6,5},{7,6},{9,8},{10,9},{11,10},{12... | collective-permute-start | bytes 30728 | tf_op jit(solution)/shard_map/ppermute | solution.py:22
  198.9 6.0 %collective-permute-start.32 = (f32[3,1,16,256]{3,2,1,0:T(8,128)S(1)}, f32[3,1,16,256]{3,2,1,0:T(8,128)S(1)}, u32[]{:S(2)}, u32[]{:S(2)}) collective-permute-start(f32[3,1,16,256]{3,2,1,0:T(8,128)S(1)} %get-tuple-element.32), channel_id=1, source_target_pairs={{8,0},{16,8},{24,16},{9,1},{17,9},{25,17},{10,2},{18,10},{26,18},{... | collective-permute-start | bytes 147464 | tf_op jit(solution)/shard_map/ppermute | solution.py:22
  200.8 6.9 %collective-permute-start.33 = (f32[3,1,16,256]{3,2,1,0:T(8,128)S(1)}, f32[3,1,16,256]{3,2,1,0:T(8,128)S(1)}, u32[]{:S(2)}, u32[]{:S(2)}) collective-permute-start(f32[3,1,16,256]{3,2,1,0:T(8,128)S(1)} %get-tuple-element.31), channel_id=1, source_target_pairs={{0,8},{8,16},{16,24},{1,9},{9,17},{17,25},{2,10},{10,18},{18,26},{... | collective-permute-start | bytes 147464 | tf_op jit(solution)/shard_map/ppermute | solution.py:19
  207.8 6.1 %collective-permute-start.34 = (f32[3,10,1,256]{3,2,1,0:T(1,128)S(1)}, f32[3,10,1,256]{3,2,1,0:T(1,128)S(1)}, u32[]{:S(2)}, u32[]{:S(2)}) collective-permute-start(f32[3,10,1,256]{3,2,1,0:T(1,128)S(1)} %get-tuple-element.24), channel_id=1, source_target_pairs={{1,0},{2,1},{3,2},{4,3},{5,4},{6,5},{7,6},{9,8},{10,9},{11,10},{12... | collective-permute-start | bytes 92168 | tf_op jit(solution)/shard_map/ppermute | solution.py:22
  215.9 6.0 %collective-permute-start.36 = (f32[3,1,16,256]{3,2,1,0:T(8,128)S(1)}, f32[3,1,16,256]{3,2,1,0:T(8,128)S(1)}, u32[]{:S(2)}, u32[]{:S(2)}) collective-permute-start(f32[3,1,16,256]{3,2,1,0:T(8,128)S(1)} %get-tuple-element.30), channel_id=1, source_target_pairs={{8,0},{16,8},{24,16},{9,1},{17,9},{25,17},{10,2},{18,10},{26,18},{... | collective-permute-start | bytes 147464 | tf_op jit(solution)/shard_map/ppermute | solution.py:22
  217.8 6.9 %collective-permute-start.37 = (f32[3,1,16,256]{3,2,1,0:T(8,128)S(1)}, f32[3,1,16,256]{3,2,1,0:T(8,128)S(1)}, u32[]{:S(2)}, u32[]{:S(2)}) collective-permute-start(f32[3,1,16,256]{3,2,1,0:T(8,128)S(1)} %get-tuple-element.29), channel_id=1, source_target_pairs={{0,8},{8,16},{16,24},{1,9},{9,17},{17,25},{2,10},{10,18},{18,26},{... | collective-permute-start | bytes 147464 | tf_op jit(solution)/shard_map/ppermute | solution.py:19
  224.8 6.3 %collective-permute-start.38 = (f32[3,10,1,256]{3,2,1,0:T(1,128)S(1)}, f32[3,10,1,256]{3,2,1,0:T(1,128)S(1)}, u32[]{:S(2)}, u32[]{:S(2)}) collective-permute-start(f32[3,10,1,256]{3,2,1,0:T(1,128)S(1)} %get-tuple-element.22), channel_id=1, source_target_pairs={{1,0},{2,1},{3,2},{4,3},{5,4},{6,5},{7,6},{9,8},{10,9},{11,10},{12... | collective-permute-start | bytes 92168 | tf_op jit(solution)/shard_map/ppermute | solution.py:22
  232.8 5.9 %collective-permute-start.40 = (f32[1,16,256]{2,1,0:T(8,128)S(1)}, f32[1,16,256]{2,1,0:T(8,128)S(1)}, u32[]{:S(2)}, u32[]{:S(2)}) collective-permute-start(f32[1,16,256]{2,1,0:T(8,128)S(1)} %get-tuple-element.72), channel_id=1, source_target_pairs={{8,0},{16,8},{24,16},{9,1},{17,9},{25,17},{10,2},{18,10},{26,18},{... | collective-permute-start | bytes 49160 | tf_op jit(solution)/shard_map/ppermute | solution.py:22
  234.7 6.5 %collective-permute-start.41 = (f32[1,16,256]{2,1,0:T(8,128)S(1)}, f32[1,16,256]{2,1,0:T(8,128)S(1)}, u32[]{:S(2)}, u32[]{:S(2)}) collective-permute-start(f32[1,16,256]{2,1,0:T(8,128)S(1)} %get-tuple-element.71), channel_id=1, source_target_pairs={{0,8},{8,16},{16,24},{1,9},{9,17},{17,25},{2,10},{10,18},{18,26},{... | collective-permute-start | bytes 49160 | tf_op jit(solution)/shard_map/ppermute | solution.py:19
  241.3 6.3 %collective-permute-start.42 = (f32[10,1,256]{2,1,0:T(1,128)S(1)}, f32[10,1,256]{2,1,0:T(1,128)S(1)}, u32[]{:S(2)}, u32[]{:S(2)}) collective-permute-start(f32[10,1,256]{2,1,0:T(1,128)S(1)} %get-tuple-element.50), channel_id=1, source_target_pairs={{1,0},{2,1},{3,2},{4,3},{5,4},{6,5},{7,6},{9,8},{10,9},{11,10},{12... | collective-permute-start | bytes 30728 | tf_op jit(solution)/shard_map/ppermute | solution.py:22
  242.6 5.8 %collective-permute-start.43 = (f32[10,1,256]{2,1,0:T(1,128)S(1)}, f32[10,1,256]{2,1,0:T(1,128)S(1)}, u32[]{:S(2)}, u32[]{:S(2)}) collective-permute-start(f32[10,1,256]{2,1,0:T(1,128)S(1)} %get-tuple-element.49), channel_id=1, source_target_pairs={{0,1},{1,2},{2,3},{3,4},{4,5},{5,6},{6,7},{8,9},{9,10},{10,11},{11... | collective-permute-start | bytes 30728 | tf_op jit(solution)/shard_map/ppermute | solution.py:19
  248.8 5.9 %collective-permute-start.44 = (f32[1,16,256]{2,1,0:T(8,128)S(1)}, f32[1,16,256]{2,1,0:T(8,128)S(1)}, u32[]{:S(2)}, u32[]{:S(2)}) collective-permute-start(f32[1,16,256]{2,1,0:T(8,128)S(1)} %get-tuple-element.70), channel_id=1, source_target_pairs={{8,0},{16,8},{24,16},{9,1},{17,9},{25,17},{10,2},{18,10},{26,18},{... | collective-permute-start | bytes 49160 | tf_op jit(solution)/shard_map/ppermute | solution.py:22
  250.7 6.5 %collective-permute-start.45 = (f32[1,16,256]{2,1,0:T(8,128)S(1)}, f32[1,16,256]{2,1,0:T(8,128)S(1)}, u32[]{:S(2)}, u32[]{:S(2)}) collective-permute-start(f32[1,16,256]{2,1,0:T(8,128)S(1)} %get-tuple-element.69), channel_id=1, source_target_pairs={{0,8},{8,16},{16,24},{1,9},{9,17},{17,25},{2,10},{10,18},{18,26},{... | collective-permute-start | bytes 49160 | tf_op jit(solution)/shard_map/ppermute | solution.py:19
  257.3 6.1 %collective-permute-start.46 = (f32[10,1,256]{2,1,0:T(1,128)S(1)}, f32[10,1,256]{2,1,0:T(1,128)S(1)}, u32[]{:S(2)}, u32[]{:S(2)}) collective-permute-start(f32[10,1,256]{2,1,0:T(1,128)S(1)} %get-tuple-element.48), channel_id=1, source_target_pairs={{1,0},{2,1},{3,2},{4,3},{5,4},{6,5},{7,6},{9,8},{10,9},{11,10},{12... | collective-permute-start | bytes 30728 | tf_op jit(solution)/shard_map/ppermute | solution.py:22
  264.7 5.9 %collective-permute-start.48 = (f32[1,16,256]{2,1,0:T(8,128)S(1)}, f32[1,16,256]{2,1,0:T(8,128)S(1)}, u32[]{:S(2)}, u32[]{:S(2)}) collective-permute-start(f32[1,16,256]{2,1,0:T(8,128)S(1)} %get-tuple-element.68), channel_id=1, source_target_pairs={{8,0},{16,8},{24,16},{9,1},{17,9},{25,17},{10,2},{18,10},{26,18},{... | collective-permute-start | bytes 49160 | tf_op jit(solution)/shard_map/ppermute | solution.py:22
  266.6 6.5 %collective-permute-start.49 = (f32[1,16,256]{2,1,0:T(8,128)S(1)}, f32[1,16,256]{2,1,0:T(8,128)S(1)}, u32[]{:S(2)}, u32[]{:S(2)}) collective-permute-start(f32[1,16,256]{2,1,0:T(8,128)S(1)} %get-tuple-element.67), channel_id=1, source_target_pairs={{0,8},{8,16},{16,24},{1,9},{9,17},{17,25},{2,10},{10,18},{18,26},{... | collective-permute-start | bytes 49160 | tf_op jit(solution)/shard_map/ppermute | solution.py:19
  273.2 6.1 %collective-permute-start.50 = (f32[10,1,256]{2,1,0:T(1,128)S(1)}, f32[10,1,256]{2,1,0:T(1,128)S(1)}, u32[]{:S(2)}, u32[]{:S(2)}) collective-permute-start(f32[10,1,256]{2,1,0:T(1,128)S(1)} %get-tuple-element.46), channel_id=1, source_target_pairs={{1,0},{2,1},{3,2},{4,3},{5,4},{6,5},{7,6},{9,8},{10,9},{11,10},{12... | collective-permute-start | bytes 30728 | tf_op jit(solution)/shard_map/ppermute | solution.py:22
  280.5 5.9 %collective-permute-start.52 = (f32[1,16,256]{2,1,0:T(8,128)S(1)}, f32[1,16,256]{2,1,0:T(8,128)S(1)}, u32[]{:S(2)}, u32[]{:S(2)}) collective-permute-start(f32[1,16,256]{2,1,0:T(8,128)S(1)} %get-tuple-element.66), channel_id=1, source_target_pairs={{8,0},{16,8},{24,16},{9,1},{17,9},{25,17},{10,2},{18,10},{26,18},{... | collective-permute-start | bytes 49160 | tf_op jit(solution)/shard_map/ppermute | solution.py:22
  282.4 6.5 %collective-permute-start.53 = (f32[1,16,256]{2,1,0:T(8,128)S(1)}, f32[1,16,256]{2,1,0:T(8,128)S(1)}, u32[]{:S(2)}, u32[]{:S(2)}) collective-permute-start(f32[1,16,256]{2,1,0:T(8,128)S(1)} %get-tuple-element.65), channel_id=1, source_target_pairs={{0,8},{8,16},{16,24},{1,9},{9,17},{17,25},{2,10},{10,18},{18,26},{... | collective-permute-start | bytes 49160 | tf_op jit(solution)/shard_map/ppermute | solution.py:19
  289.0 29.2 %collective-permute-start.54 = (f32[10,1,256]{2,1,0:T(1,128)S(1)}, f32[10,1,256]{2,1,0:T(1,128)S(1)}, u32[]{:S(2)}, u32[]{:S(2)}) collective-permute-start(f32[10,1,256]{2,1,0:T(1,128)S(1)} %get-tuple-element.44), channel_id=1, source_target_pairs={{1,0},{2,1},{3,2},{4,3},{5,4},{6,5},{7,6},{9,8},{10,9},{11,10},{12... | collective-permute-start | bytes 30728 | tf_op jit(solution)/shard_map/ppermute | solution.py:22
  290.3 27.9 %collective-permute-start.55 = (f32[10,1,256]{2,1,0:T(1,128)S(1)}, f32[10,1,256]{2,1,0:T(1,128)S(1)}, u32[]{:S(2)}, u32[]{:S(2)}) collective-permute-start(f32[10,1,256]{2,1,0:T(1,128)S(1)} %get-tuple-element.43), channel_id=1, source_target_pairs={{0,1},{1,2},{2,3},{3,4},{4,5},{5,6},{6,7},{8,9},{9,10},{10,11},{11... | collective-permute-start | bytes 30728 | tf_op jit(solution)/shard_map/ppermute | solution.py:19
  345.3 13.1 %all-to-all-start.2 = ((f32[1,1,8,4,512]{4,3,1,0,2:T(4,128)}), f32[1,1,8,4,512]{4,3,1,0,2:T(4,128)S(1)}, u32[]{:S(2)}, u32[]{:S(2)}) async-start(f32[1,1,8,4,512]{4,3,1,0,2:T(4,128)} %pad_maximum_fusion.105), calls=%async_computation.2 | async-start | bytes 131072 | tf_op jit(solution)/shard_map/all_to_all | solution.py:135
  (35 other events, 363.9 us)
where the time goes:
time: 361 us; the launch traced here: 359 us
  starting transfers between devices  178 us (49%)
  local copies, waits for them, and re-layouts  68.4 us (19%)
  other arithmetic  63.4 us (18%)
  waiting for transfers between devices  47.2 us (13%)
    ppermute x28, starting transfers between devices, extended(): lax.ppermute(lax.slice_in_dim(block, block.shape[dim] - width, None, axis...  110 us
    ppermute x28, starting transfers between devices, extended(): lax.ppermute(lax.slice_in_dim(block, 0, width, axis=dim), axis, backward)  51.1 us
    ppermute x28, waiting for transfers between devices, extended(): lax.ppermute(lax.slice_in_dim(block, block.shape[dim] - width, None, axis...  38.8 us
    scatter-add x1, other arithmetic, per_device(): jax.ops.segment_sum(carried, target_field, num_segments=grid_cells)  29.5 us
    gather x1, local copies, waits for them, and re-layouts, per_device(): flattened_voids[target_field].reshape(slot_shape_factors)  23 us
    scatter-add x1, other arithmetic, per_device(): jax.ops.segment_sum(got_vol.reshape(-1), target_field, num_segments=grid_...  21.9 us
    gather x1, local copies, waits for them, and re-layouts, per_device(): flat_vel[:, target_field].reshape((3,) + slot_shape_factors)  16.5 us
    reshape x1, local copies, waits for them, and re-layouts, per_device(): jax.ops.segment_sum(carried, target_field, num_segments=grid_cells)  9.97 us
  transfers between devices with their start and end apart: 59, of which 26 were waited for; matrix products, arithmetic and copies ran while one was open for 25% of the time, Pallas kernels for 0%

commit v1 on v0

--- a/solution.py
+++ b/solution.py
@@ -2,6 +2,7 @@
 import jax.numpy as jnp
 from jax import lax
 from jax.sharding import PartitionSpec as P
+from jax.lax import all_to_all, axis_size
 
 STEPS = 2
 SWEEPS = 4
@@ -132,7 +133,14 @@
     )
     cell_void_fraction = flattened_voids[target_field].reshape(slot_shape_factors)
     coupled_state = jnp.concatenate([cell_flow_speed, cell_void_fraction[..., None, :]], axis=3)
-    back = lax.all_to_all(coupled_state, "gy", split_axis=2, concat_axis=2, tiled=True)
+
+    def follow_sheet(z, along_axis):
+        known = jnp.stack(jnp.split(z, axis_size(along_axis), axis=2), axis=0)
+        return jnp.concatenate(
+            all_to_all(known, axis_name=along_axis, split_axis=0, concat_axis=0), axis=2
+        )
+
+    back = follow_sheet(coupled_state, "gy")
     drag = (
         grain_volume[..., None, :]
         * drag_coefficient

time: 361 us -> 366 us (1.014)
  other arithmetic: 63.4 us -> 67.5 us
    unnamed x0 -> x7, other arithmetic: none -> 4.23 us
where the time goes in v1:
time: 366 us; the launch traced here: 363 us
  starting transfers between devices  178 us (49%)
  local copies, waits for them, and re-layouts  68.4 us (19%)
  other arithmetic  67.5 us (18%)
  waiting for transfers between devices  47.2 us (13%)
    ppermute x28, starting transfers between devices, extended(): lax.ppermute(lax.slice_in_dim(block, block.shape[dim] - width, None, axis...  110 us
    ppermute x28, starting transfers between devices, extended(): lax.ppermute(lax.slice_in_dim(block, 0, width, axis=dim), axis, backward)  51.1 us
    ppermute x28, waiting for transfers between devices, extended(): lax.ppermute(lax.slice_in_dim(block, block.shape[dim] - width, None, axis...  38.8 us
    scatter-add x1, other arithmetic, per_device(): jax.ops.segment_sum(carried, target_field, num_segments=grid_cells)  29.5 us
    gather x1, local copies, waits for them, and re-layouts, per_device(): flattened_voids[target_field].reshape(slot_shape_factors)  23 us
    scatter-add x1, other arithmetic, per_device(): jax.ops.segment_sum(got_vol.reshape(-1), target_field, num_segments=grid_...  21.9 us
    gather x1, local copies, waits for them, and re-layouts, per_device(): flat_vel[:, target_field].reshape((3,) + slot_shape_factors)  16.5 us
    reshape x1, local copies, waits for them, and re-layouts, per_device(): jax.ops.segment_sum(carried, target_field, num_segments=grid_cells)  9.97 us
  transfers between devices with their start and end apart: 59, of which 26 were waited for; matrix products, arithmetic and copies ran while one was open for 25% of the time, Pallas kernels for 0%

profile of v1, /device:TPU:4, one launch (start us, length us, event | category | flops | bytes accessed | tf_op | source)
XLA Modules:
  0.0 363.3 jit_solution(13596238236922394150)
XLA Ops:
  3.6 4.9 %all-to-all-start.1 = ((f32[1,1,8,4,512]{4,3,1,0,2:T(4,128)}), f32[1,1,8,4,512]{4,3,1,0,2:T(4,128)S(1)}, u32[]{:S(2)}, u32[]{:S(2)}) async-start(f32[1,1,8,4,512]{4,3,1,0,2:T(4,128)} %pad_maximum_fusion.104), calls=%async_computation.1 | async-start | bytes 131072 | tf_op jit(solution)/shard_map/all_to_all | solution.py:97
  9.2 3.4 collective-permute-start.9
  15.4 4.8 %collective-permute-start.1 = (f32[3,1,16,256]{3,2,1,0:T(8,128)S(1)}, f32[3,1,16,256]{3,2,1,0:T(8,128)S(1)}, u32[]{:S(2)}, u32[]{:S(2)}) collective-permute-start(f32[3,1,16,256]{3,2,1,0:T(8,128)S(1)} %get-tuple-element.35), channel_id=1, source_target_pairs={{8,0},{16,8},{24,16},{9,1},{17,9},{25,17},{10,2},{18,10},{26,18},{... | collective-permute-start | bytes 147464 | tf_op jit(solution)/shard_map/ppermute | solution.py:23
  25.9 5.1 %all-to-all-start = ((s32[1,1,8,512]{3,1,0,2:T(1,128)}), s32[1,1,8,512]{3,1,0,2:T(1,128)S(1)}, u32[]{:S(2)}, u32[]{:S(2)}) async-start(s32[1,1,8,512]{3,1,0,2:T(1,128)} %copy.25), calls=%async_computation | async-start | bytes 32768 | tf_op jit(solution)/shard_map/all_to_all | solution.py:96
  32.4 3.0 collective-permute-start.7
  36.7 21.9 %scatter_custom_fusion = f32[32768]{0:T(1024)S(1)} fusion(s32[4096]{0:T(1024)S(1)} %bitcast.88, f32[4096]{0:T(1024)S(1)} %bitcast.92, f32[]{:T(128)} %constant.10.clone.1), kind=kCustom, calls=%fused_computation.374 | custom fusion | flops 4096 | bytes 131076 | tf_op jit(solution)/shard_map/scatter-add | solution.py:102
  59.4 3.3 collective-permute-start
  65.9 3.5 collective-permute-done.2
  70.8 3.0 collective-permute-start.6
  75.8 29.5 %scatter_custom_fusion.1 = f32[32768,3]{1,0:T(8,128)} fusion(s32[4096]{0:T(1024)S(1)} %bitcast.89, f32[4096,3]{1,0:T(8,128)} %copy.29, f32[]{:T(128)} %constant.10.clone.1), kind=kCustom, calls=%fused_computation.4 | custom fusion | flops 12288 | bytes 393728 | tf_op jit(solution)/shard_map/scatter-add | solution.py:105
  105.4 10.0 %copy.30 = f32[3,8,16,256]{3,2,1,0:T(8,128)S(1)} copy(f32[3,8,16,256]{0,3,2,1:T(8,128)} %bitcast.64) | data formatting | bytes 786432 | tf_op jit(solution)/shard_map/reshape | solution.py:105
  120.3 3.9 %collective-permute-start.13 = (f32[3,1,16,256]{3,2,1,0:T(8,128)S(1)}, f32[3,1,16,256]{3,2,1,0:T(8,128)S(1)}, u32[]{:S(2)}, u32[]{:S(2)}) collective-permute-start(f32[3,1,16,256]{3,2,1,0:T(8,128)S(1)} %get-tuple-element.33), channel_id=1, source_target_pairs={{0,8},{8,16},{16,24},{1,9},{9,17},{17,25},{2,10},{10,18},{18,26},{... | collective-permute-start | bytes 147464 | tf_op jit(solution)/shard_map/ppermute | solution.py:20
  125.6 3.0 collective-permute-start.11
  130.0 4.0 %collective-permute-start.15 = (f32[3,10,1,256]{3,2,1,0:T(1,128)S(1)}, f32[3,10,1,256]{3,2,1,0:T(1,128)S(1)}, u32[]{:S(2)}, u32[]{:S(2)}) collective-permute-start(f32[3,10,1,256]{3,2,1,0:T(1,128)S(1)} %get-tuple-element.25), channel_id=1, source_target_pairs={{0,1},{1,2},{2,3},{3,4},{4,5},{5,6},{6,7},{8,9},{9,10},{10,11},{11... | collective-permute-start | bytes 92168 | tf_op jit(solution)/shard_map/ppermute | solution.py:20
  135.8 3.1 collective-permute-start.16
  139.0 2.7 collective-permute-start.17
  141.7 3.8 %collective-permute-done.17 = f32[1,16,256]{2,1,0:T(8,128)S(1)} collective-permute-done((f32[1,16,256]{2,1,0:T(8,128)S(1)}, f32[1,16,256]{2,1,0:T(8,128)S(1)}, u32[]{:S(2)}, u32[]{:S(2)}) %collective-permute-start.17) | collective-permute-done | bytes 16416 | tf_op jit(solution)/shard_map/ppermute | solution.py:20
  146.8 3.0 collective-permute-start.19
  153.0 3.9 %collective-permute-start.21 = (f32[1,16,256]{2,1,0:T(8,128)S(1)}, f32[1,16,256]{2,1,0:T(8,128)S(1)}, u32[]{:S(2)}, u32[]{:S(2)}) collective-permute-start(f32[1,16,256]{2,1,0:T(8,128)S(1)} %get-tuple-element.77), channel_id=1, source_target_pairs={{0,8},{8,16},{16,24},{1,9},{9,17},{17,25},{2,10},{10,18},{18,26},{... | collective-permute-start | bytes 49160 | tf_op jit(solution)/shard_map/ppermute | solution.py:20
  160.9 5.2 %collective-permute-start.23 = (f32[10,1,256]{2,1,0:T(1,128)S(1)}, f32[10,1,256]{2,1,0:T(1,128)S(1)}, u32[]{:S(2)}, u32[]{:S(2)}) collective-permute-start(f32[10,1,256]{2,1,0:T(1,128)S(1)} %get-tuple-element.57), channel_id=1, source_target_pairs={{0,1},{1,2},{2,3},{3,4},{4,5},{5,6},{6,7},{8,9},{9,10},{10,11},{11... | collective-permute-start | bytes 30728 | tf_op jit(solution)/shard_map/ppermute | solution.py:20
  169.1 3.9 %collective-permute-start.25 = (f32[1,16,256]{2,1,0:T(8,128)S(1)}, f32[1,16,256]{2,1,0:T(8,128)S(1)}, u32[]{:S(2)}, u32[]{:S(2)}) collective-permute-start(f32[1,16,256]{2,1,0:T(8,128)S(1)} %get-tuple-element.75), channel_id=1, source_target_pairs={{0,8},{8,16},{16,24},{1,9},{9,17},{17,25},{2,10},{10,18},{18,26},{... | collective-permute-start | bytes 49160 | tf_op jit(solution)/shard_map/ppermute | solution.py:20
  173.0 2.6 collective-permute-done.25
  177.0 4.8 %collective-permute-start.27 = (f32[10,1,256]{2,1,0:T(1,128)S(1)}, f32[10,1,256]{2,1,0:T(1,128)S(1)}, u32[]{:S(2)}, u32[]{:S(2)}) collective-permute-start(f32[10,1,256]{2,1,0:T(1,128)S(1)} %get-tuple-element.55), channel_id=1, source_target_pairs={{0,1},{1,2},{2,3},{3,4},{4,5},{5,6},{6,7},{8,9},{9,10},{10,11},{11... | collective-permute-start | bytes 30728 | tf_op jit(solution)/shard_map/ppermute | solution.py:20
  184.9 3.9 %collective-permute-start.29 = (f32[1,16,256]{2,1,0:T(8,128)S(1)}, f32[1,16,256]{2,1,0:T(8,128)S(1)}, u32[]{:S(2)}, u32[]{:S(2)}) collective-permute-start(f32[1,16,256]{2,1,0:T(8,128)S(1)} %get-tuple-element.73), channel_id=1, source_target_pairs={{0,8},{8,16},{16,24},{1,9},{9,17},{17,25},{2,10},{10,18},{18,26},{... | collective-permute-start | bytes 49160 | tf_op jit(solution)/shard_map/ppermute | solution.py:20
  188.8 2.6 collective-permute-done.29
  192.8 4.8 %collective-permute-start.31 = (f32[10,1,256]{2,1,0:T(1,128)S(1)}, f32[10,1,256]{2,1,0:T(1,128)S(1)}, u32[]{:S(2)}, u32[]{:S(2)}) collective-permute-start(f32[10,1,256]{2,1,0:T(1,128)S(1)} %get-tuple-element.53), channel_id=1, source_target_pairs={{0,1},{1,2},{2,3},{3,4},{4,5},{5,6},{6,7},{8,9},{9,10},{10,11},{11... | collective-permute-start | bytes 30728 | tf_op jit(solution)/shard_map/ppermute | solution.py:20
  200.8 3.9 %collective-permute-start.33 = (f32[3,1,16,256]{3,2,1,0:T(8,128)S(1)}, f32[3,1,16,256]{3,2,1,0:T(8,128)S(1)}, u32[]{:S(2)}, u32[]{:S(2)}) collective-permute-start(f32[3,1,16,256]{3,2,1,0:T(8,128)S(1)} %get-tuple-element.31), channel_id=1, source_target_pairs={{0,8},{8,16},{16,24},{1,9},{9,17},{17,25},{2,10},{10,18},{18,26},{... | collective-permute-start | bytes 147464 | tf_op jit(solution)/shard_map/ppermute | solution.py:20
  204.9 2.8 collective-permute-done.33
  209.1 4.8 %collective-permute-start.35 = (f32[3,10,1,256]{3,2,1,0:T(1,128)S(1)}, f32[3,10,1,256]{3,2,1,0:T(1,128)S(1)}, u32[]{:S(2)}, u32[]{:S(2)}) collective-permute-start(f32[3,10,1,256]{3,2,1,0:T(1,128)S(1)} %get-tuple-element.23), channel_id=1, source_target_pairs={{0,1},{1,2},{2,3},{3,4},{4,5},{5,6},{6,7},{8,9},{9,10},{10,11},{11... | collective-permute-start | bytes 92168 | tf_op jit(solution)/shard_map/ppermute | solution.py:20
  217.8 3.9 %collective-permute-start.37 = (f32[3,1,16,256]{3,2,1,0:T(8,128)S(1)}, f32[3,1,16,256]{3,2,1,0:T(8,128)S(1)}, u32[]{:S(2)}, u32[]{:S(2)}) collective-permute-start(f32[3,1,16,256]{3,2,1,0:T(8,128)S(1)} %get-tuple-element.29), channel_id=1, source_target_pairs={{0,8},{8,16},{16,24},{1,9},{9,17},{17,25},{2,10},{10,18},{18,26},{... | collective-permute-start | bytes 147464 | tf_op jit(solution)/shard_map/ppermute | solution.py:20
  221.9 2.8 collective-permute-done.37
  226.1 5.0 %collective-permute-start.39 = (f32[3,10,1,256]{3,2,1,0:T(1,128)S(1)}, f32[3,10,1,256]{3,2,1,0:T(1,128)S(1)}, u32[]{:S(2)}, u32[]{:S(2)}) collective-permute-start(f32[3,10,1,256]{3,2,1,0:T(1,128)S(1)} %get-tuple-element.21), channel_id=1, source_target_pairs={{0,1},{1,2},{2,3},{3,4},{4,5},{5,6},{6,7},{8,9},{9,10},{10,11},{11... | collective-permute-start | bytes 92168 | tf_op jit(solution)/shard_map/ppermute | solution.py:20
  234.7 3.9 %collective-permute-start.41 = (f32[1,16,256]{2,1,0:T(8,128)S(1)}, f32[1,16,256]{2,1,0:T(8,128)S(1)}, u32[]{:S(2)}, u32[]{:S(2)}) collective-permute-start(f32[1,16,256]{2,1,0:T(8,128)S(1)} %get-tuple-element.71), channel_id=1, source_target_pairs={{0,8},{8,16},{16,24},{1,9},{9,17},{17,25},{2,10},{10,18},{18,26},{... | collective-permute-start | bytes 49160 | tf_op jit(solution)/shard_map/ppermute | solution.py:20
  242.6 5.0 %collective-permute-start.43 = (f32[10,1,256]{2,1,0:T(1,128)S(1)}, f32[10,1,256]{2,1,0:T(1,128)S(1)}, u32[]{:S(2)}, u32[]{:S(2)}) collective-permute-start(f32[10,1,256]{2,1,0:T(1,128)S(1)} %get-tuple-element.49), channel_id=1, source_target_pairs={{0,1},{1,2},{2,3},{3,4},{4,5},{5,6},{6,7},{8,9},{9,10},{10,11},{11... | collective-permute-start | bytes 30728 | tf_op jit(solution)/shard_map/ppermute | solution.py:20
  250.7 3.9 %collective-permute-start.45 = (f32[1,16,256]{2,1,0:T(8,128)S(1)}, f32[1,16,256]{2,1,0:T(8,128)S(1)}, u32[]{:S(2)}, u32[]{:S(2)}) collective-permute-start(f32[1,16,256]{2,1,0:T(8,128)S(1)} %get-tuple-element.69), channel_id=1, source_target_pairs={{0,8},{8,16},{16,24},{1,9},{9,17},{17,25},{2,10},{10,18},{18,26},{... | collective-permute-start | bytes 49160 | tf_op jit(solution)/shard_map/ppermute | solution.py:20
  254.7 2.6 collective-permute-done.45
  258.6 4.8 %collective-permute-start.47 = (f32[10,1,256]{2,1,0:T(1,128)S(1)}, f32[10,1,256]{2,1,0:T(1,128)S(1)}, u32[]{:S(2)}, u32[]{:S(2)}) collective-permute-start(f32[10,1,256]{2,1,0:T(1,128)S(1)} %get-tuple-element.47), channel_id=1, source_target_pairs={{0,1},{1,2},{2,3},{3,4},{4,5},{5,6},{6,7},{8,9},{9,10},{10,11},{11... | collective-permute-start | bytes 30728 | tf_op jit(solution)/shard_map/ppermute | solution.py:20
  266.6 3.9 %collective-permute-start.49 = (f32[1,16,256]{2,1,0:T(8,128)S(1)}, f32[1,16,256]{2,1,0:T(8,128)S(1)}, u32[]{:S(2)}, u32[]{:S(2)}) collective-permute-start(f32[1,16,256]{2,1,0:T(8,128)S(1)} %get-tuple-element.67), channel_id=1, source_target_pairs={{0,8},{8,16},{16,24},{1,9},{9,17},{17,25},{2,10},{10,18},{18,26},{... | collective-permute-start | bytes 49160 | tf_op jit(solution)/shard_map/ppermute | solution.py:20
  270.5 2.6 collective-permute-done.49
  274.5 4.8 %collective-permute-start.51 = (f32[10,1,256]{2,1,0:T(1,128)S(1)}, f32[10,1,256]{2,1,0:T(1,128)S(1)}, u32[]{:S(2)}, u32[]{:S(2)}) collective-permute-start(f32[10,1,256]{2,1,0:T(1,128)S(1)} %get-tuple-element.45), channel_id=1, source_target_pairs={{0,1},{1,2},{2,3},{3,4},{4,5},{5,6},{6,7},{8,9},{9,10},{10,11},{11... | collective-permute-start | bytes 30728 | tf_op jit(solution)/shard_map/ppermute | solution.py:20
  282.4 3.9 %collective-permute-start.53 = (f32[1,16,256]{2,1,0:T(8,128)S(1)}, f32[1,16,256]{2,1,0:T(8,128)S(1)}, u32[]{:S(2)}, u32[]{:S(2)}) collective-permute-start(f32[1,16,256]{2,1,0:T(8,128)S(1)} %get-tuple-element.65), channel_id=1, source_target_pairs={{0,8},{8,16},{16,24},{1,9},{9,17},{17,25},{2,10},{10,18},{18,26},{... | collective-permute-start | bytes 49160 | tf_op jit(solution)/shard_map/ppermute | solution.py:20
  286.4 2.6 collective-permute-done.53
  290.3 4.8 %collective-permute-start.55 = (f32[10,1,256]{2,1,0:T(1,128)S(1)}, f32[10,1,256]{2,1,0:T(1,128)S(1)}, u32[]{:S(2)}, u32[]{:S(2)}) collective-permute-start(f32[10,1,256]{2,1,0:T(1,128)S(1)} %get-tuple-element.43), channel_id=1, source_target_pairs={{0,1},{1,2},{2,3},{3,4},{4,5},{5,6},{6,7},{8,9},{9,10},{10,11},{11... | collective-permute-start | bytes 30728 | tf_op jit(solution)/shard_map/ppermute | solution.py:20
  295.1 23.0 %gather_fusion.1 = f32[4096]{0:T(1024)S(1)} fusion(f32[32768]{0:T(1024)S(1)} %subtract_maximum_fusion, s32[4096]{0:T(1024)S(1)} %broadcast_clamp_fusion), kind=kCustom, calls=%fused_computation.1 | custom fusion | bytes 49152 | tf_op jit(solution)/shard_map/gather | solution.py:134
  318.7 8.7 %copy.32 = f32[3,8,16,256]{0,3,2,1:T(8,128)} copy(f32[3,8,16,256]{3,2,1,0:T(8,128)S(1)} %fusion.54) | data formatting | bytes 786432 | tf_op jit(solution)/shard_map/sub | solution.py:127
  327.4 16.5 %gather_fusion = f32[4096,3]{1,0:T(8,128)S(1)} fusion(f32[3,32768]{0,1:T(8,128)} %bitcast.65, s32[4096]{0:T(1024)S(1)} %broadcast_clamp_fusion), kind=kCustom, calls=%fused_computation | custom fusion | bytes 114688 | tf_op jit(solution)/shard_map/gather | solution.py:132
  349.4 7.2 %all-to-all-start.2 = ((f32[8,1,1,1,4,512]{5,4,3,2,1,0:T(4,128)}), f32[8,1,1,1,4,512]{5,4,3,2,1,0:T(4,128)S(1)}, u32[]{:S(2)}, u32[]{:S(2)}) async-start(f32[8,1,1,1,4,512]{5,4,3,2,1,0:T(4,128)} %constant_dynamic-update-slice_fusion.6), calls=%async_computation.2 | async-start | bytes 131072 | tf_op jit(solution)/shard_map/all_to_all | solution.py:140
  356.6 5.9 %all-to-all-done.2 = f32[8,1,1,1,4,512]{5,4,3,2,1,0:T(4,128)S(1)} async-done(((f32[8,1,1,1,4,512]{5,4,3,2,1,0:T(4,128)}), f32[8,1,1,1,4,512]{5,4,3,2,1,0:T(4,128)S(1)}, u32[]{:S(2)}, u32[]{:S(2)}) %all-to-all-start.2) | async-done | bytes 65568 | tf_op jit(solution)/shard_map/all_to_all | solution.py:140
  (216 shorter events, 85.7 us)
Async XLA Ops:
  3.6 22.3 %all-to-all-start.1 = ((f32[1,1,8,4,512]{4,3,1,0,2:T(4,128)}), f32[1,1,8,4,512]{4,3,1,0,2:T(4,128)S(1)}, u32[]{:S(2)}, u32[]{:S(2)}) async-start(f32[1,1,8,4,512]{4,3,1,0,2:T(4,128)} %pad_maximum_fusion.104), calls=%async_computation.1 | async-start | bytes 131072 | tf_op jit(solution)/shard_map/all_to_all | solution.py:97
  9.2 14.8 %collective-permute-start.9 = (f32[1,16,256]{2,1,0:T(8,128)S(1)}, f32[1,16,256]{2,1,0:T(8,128)S(1)}, u32[]{:S(2)}, u32[]{:S(2)}) collective-permute-start(f32[1,16,256]{2,1,0:T(8,128)S(1)} %get-tuple-element.82), channel_id=1, source_target_pairs={{0,8},{8,16},{16,24},{1,9},{9,17},{17,25},{2,10},{10,18},{18,26},{... | collective-permute-start | bytes 49160 | tf_op jit(solution)/shard_map/ppermute | solution.py:20
  13.4 12.4 %collective-permute-start.3 = (f32[3,1,16,256]{3,2,1,0:T(8,128)S(1)}, f32[3,1,16,256]{3,2,1,0:T(8,128)S(1)}, u32[]{:S(2)}, u32[]{:S(2)}) collective-permute-start(f32[3,1,16,256]{3,2,1,0:T(8,128)S(1)} %get-tuple-element.36), channel_id=1, source_target_pairs={{0,8},{8,16},{16,24},{1,9},{9,17},{17,25},{2,10},{10,18},{18,26},{... | collective-permute-start | bytes 147464 | tf_op jit(solution)/shard_map/ppermute | solution.py:20
  15.4 10.5 %collective-permute-start.1 = (f32[3,1,16,256]{3,2,1,0:T(8,128)S(1)}, f32[3,1,16,256]{3,2,1,0:T(8,128)S(1)}, u32[]{:S(2)}, u32[]{:S(2)}) collective-permute-start(f32[3,1,16,256]{3,2,1,0:T(8,128)S(1)} %get-tuple-element.35), channel_id=1, source_target_pairs={{8,0},{16,8},{24,16},{9,1},{17,9},{25,17},{10,2},{18,10},{26,18},{... | collective-permute-start | bytes 147464 | tf_op jit(solution)/shard_map/ppermute | solution.py:23
  25.9 10.8 %all-to-all-start = ((s32[1,1,8,512]{3,1,0,2:T(1,128)}), s32[1,1,8,512]{3,1,0,2:T(1,128)S(1)}, u32[]{:S(2)}, u32[]{:S(2)}) async-start(s32[1,1,8,512]{3,1,0,2:T(1,128)} %copy.25), calls=%async_computation | async-start | bytes 32768 | tf_op jit(solution)/shard_map/all_to_all | solution.py:96
  31.1 34.2 %collective-permute-start.5 = (f32[3,10,1,256]{3,2,1,0:T(1,128)S(1)}, f32[3,10,1,256]{3,2,1,0:T(1,128)S(1)}, u32[]{:S(2)}, u32[]{:S(2)}) collective-permute-start(f32[3,10,1,256]{3,2,1,0:T(1,128)S(1)} %get-tuple-element.28), channel_id=1, source_target_pairs={{1,0},{2,1},{3,2},{4,3},{5,4},{6,5},{7,6},{9,8},{10,9},{11,10},{12... | collective-permute-start | bytes 92168 | tf_op jit(solution)/shard_map/ppermute | solution.py:23
  32.4 32.9 %collective-permute-start.7 = (f32[3,10,1,256]{3,2,1,0:T(1,128)S(1)}, f32[3,10,1,256]{3,2,1,0:T(1,128)S(1)}, u32[]{:S(2)}, u32[]{:S(2)}) collective-permute-start(f32[3,10,1,256]{3,2,1,0:T(1,128)S(1)} %get-tuple-element.27), channel_id=1, source_target_pairs={{0,1},{1,2},{2,3},{3,4},{4,5},{5,6},{6,7},{8,9},{9,10},{10,11},{11... | collective-permute-start | bytes 92168 | tf_op jit(solution)/shard_map/ppermute | solution.py:20
  59.4 6.5 %collective-permute-start = (f32[2,16,256]{2,1,0:T(8,128)S(1)}, f32[2,16,256]{2,1,0:T(8,128)S(1)}, u32[]{:S(2)}, u32[]{:S(2)}) collective-permute-start(f32[2,16,256]{2,1,0:T(8,128)S(1)} %get-tuple-element.84), channel_id=1, source_target_pairs={{8,0},{16,8},{24,16},{9,1},{17,9},{25,17},{10,2},{18,10},{26,18},{... | collective-permute-start | bytes 98312 | tf_op jit(solution)/shard_map/ppermute | solution.py:23
  62.8 6.7 %collective-permute-start.2 = (f32[2,16,256]{2,1,0:T(8,128)S(1)}, f32[2,16,256]{2,1,0:T(8,128)S(1)}, u32[]{:S(2)}, u32[]{:S(2)}) collective-permute-start(f32[2,16,256]{2,1,0:T(8,128)S(1)} %get-tuple-element.83), channel_id=1, source_target_pairs={{0,8},{8,16},{16,24},{1,9},{9,17},{17,25},{2,10},{10,18},{18,26},{... | collective-permute-start | bytes 98312 | tf_op jit(solution)/shard_map/ppermute | solution.py:20
  69.5 45.9 %collective-permute-start.4 = (f32[12,2,256]{2,1,0:T(2,128)S(1)}, f32[12,2,256]{2,1,0:T(2,128)S(1)}, u32[]{:S(2)}, u32[]{:S(2)}) collective-permute-start(f32[12,2,256]{2,1,0:T(2,128)S(1)} %get-tuple-element.40), channel_id=1, source_target_pairs={{1,0},{2,1},{3,2},{4,3},{5,4},{6,5},{7,6},{9,8},{10,9},{11,10},{12... | collective-permute-start | bytes 73736 | tf_op jit(solution)/shard_map/ppermute | solution.py:23
  70.8 44.6 %collective-permute-start.6 = (f32[12,2,256]{2,1,0:T(2,128)S(1)}, f32[12,2,256]{2,1,0:T(2,128)S(1)}, u32[]{:S(2)}, u32[]{:S(2)}) collective-permute-start(f32[12,2,256]{2,1,0:T(2,128)S(1)} %get-tuple-element.39), channel_id=1, source_target_pairs={{0,1},{1,2},{2,3},{3,4},{4,5},{5,6},{6,7},{8,9},{9,10},{10,11},{11... | collective-permute-start | bytes 73736 | tf_op jit(solution)/shard_map/ppermute | solution.py:20
  118.4 10.2 %collective-permute-start.12 = (f32[3,1,16,256]{3,2,1,0:T(8,128)S(1)}, f32[3,1,16,256]{3,2,1,0:T(8,128)S(1)}, u32[]{:S(2)}, u32[]{:S(2)}) collective-permute-start(f32[3,1,16,256]{3,2,1,0:T(8,128)S(1)} %get-tuple-element.34), channel_id=1, source_target_pairs={{8,0},{16,8},{24,16},{9,1},{17,9},{25,17},{10,2},{18,10},{26,18},{... | collective-permute-start | bytes 147464 | tf_op jit(solution)/shard_map/ppermute | solution.py:23
  120.3 8.3 %collective-permute-start.13 = (f32[3,1,16,256]{3,2,1,0:T(8,128)S(1)}, f32[3,1,16,256]{3,2,1,0:T(8,128)S(1)}, u32[]{:S(2)}, u32[]{:S(2)}) collective-permute-start(f32[3,1,16,256]{3,2,1,0:T(8,128)S(1)} %get-tuple-element.33), channel_id=1, source_target_pairs={{0,8},{8,16},{16,24},{1,9},{9,17},{17,25},{2,10},{10,18},{18,26},{... | collective-permute-start | bytes 147464 | tf_op jit(solution)/shard_map/ppermute | solution.py:20
  124.3 9.8 %collective-permute-start.10 = (f32[10,1,256]{2,1,0:T(1,128)S(1)}, f32[10,1,256]{2,1,0:T(1,128)S(1)}, u32[]{:S(2)}, u32[]{:S(2)}) collective-permute-start(f32[10,1,256]{2,1,0:T(1,128)S(1)} %get-tuple-element.62), channel_id=1, source_target_pairs={{1,0},{2,1},{3,2},{4,3},{5,4},{6,5},{7,6},{9,8},{10,9},{11,10},{12... | collective-permute-start | bytes 30728 | tf_op jit(solution)/shard_map/ppermute | solution.py:23
  125.6 8.5 %collective-permute-start.11 = (f32[10,1,256]{2,1,0:T(1,128)S(1)}, f32[10,1,256]{2,1,0:T(1,128)S(1)}, u32[]{:S(2)}, u32[]{:S(2)}) collective-permute-start(f32[10,1,256]{2,1,0:T(1,128)S(1)} %get-tuple-element.61), channel_id=1, source_target_pairs={{0,1},{1,2},{2,3},{3,4},{4,5},{5,6},{6,7},{8,9},{9,10},{10,11},{11... | collective-permute-start | bytes 30728 | tf_op jit(solution)/shard_map/ppermute | solution.py:20
  135.8 5.9 %collective-permute-start.16 = (f32[1,16,256]{2,1,0:T(8,128)S(1)}, f32[1,16,256]{2,1,0:T(8,128)S(1)}, u32[]{:S(2)}, u32[]{:S(2)}) collective-permute-start(f32[1,16,256]{2,1,0:T(8,128)S(1)} %get-tuple-element.80), channel_id=1, source_target_pairs={{8,0},{16,8},{24,16},{9,1},{17,9},{25,17},{10,2},{18,10},{26,18},{... | collective-permute-start | bytes 49160 | tf_op jit(solution)/shard_map/ppermute | solution.py:23
  139.0 6.5 %collective-permute-start.17 = (f32[1,16,256]{2,1,0:T(8,128)S(1)}, f32[1,16,256]{2,1,0:T(8,128)S(1)}, u32[]{:S(2)}, u32[]{:S(2)}) collective-permute-start(f32[1,16,256]{2,1,0:T(8,128)S(1)} %get-tuple-element.79), channel_id=1, source_target_pairs={{0,8},{8,16},{16,24},{1,9},{9,17},{17,25},{2,10},{10,18},{18,26},{... | collective-permute-start | bytes 49160 | tf_op jit(solution)/shard_map/ppermute | solution.py:20
  151.1 5.9 %collective-permute-start.20 = (f32[1,16,256]{2,1,0:T(8,128)S(1)}, f32[1,16,256]{2,1,0:T(8,128)S(1)}, u32[]{:S(2)}, u32[]{:S(2)}) collective-permute-start(f32[1,16,256]{2,1,0:T(8,128)S(1)} %get-tuple-element.78), channel_id=1, source_target_pairs={{8,0},{16,8},{24,16},{9,1},{17,9},{25,17},{10,2},{18,10},{26,18},{... | collective-permute-start | bytes 49160 | tf_op jit(solution)/shard_map/ppermute | solution.py:23
  153.0 6.5 %collective-permute-start.21 = (f32[1,16,256]{2,1,0:T(8,128)S(1)}, f32[1,16,256]{2,1,0:T(8,128)S(1)}, u32[]{:S(2)}, u32[]{:S(2)}) collective-permute-start(f32[1,16,256]{2,1,0:T(8,128)S(1)} %get-tuple-element.77), channel_id=1, source_target_pairs={{0,8},{8,16},{16,24},{1,9},{9,17},{17,25},{2,10},{10,18},{18,26},{... | collective-permute-start | bytes 49160 | tf_op jit(solution)/shard_map/ppermute | solution.py:20
  159.6 6.6 %collective-permute-start.22 = (f32[10,1,256]{2,1,0:T(1,128)S(1)}, f32[10,1,256]{2,1,0:T(1,128)S(1)}, u32[]{:S(2)}, u32[]{:S(2)}) collective-permute-start(f32[10,1,256]{2,1,0:T(1,128)S(1)} %get-tuple-element.58), channel_id=1, source_target_pairs={{1,0},{2,1},{3,2},{4,3},{5,4},{6,5},{7,6},{9,8},{10,9},{11,10},{12... | collective-permute-start | bytes 30728 | tf_op jit(solution)/shard_map/ppermute | solution.py:23
  160.9 5.9 %collective-permute-start.23 = (f32[10,1,256]{2,1,0:T(1,128)S(1)}, f32[10,1,256]{2,1,0:T(1,128)S(1)}, u32[]{:S(2)}, u32[]{:S(2)}) collective-permute-start(f32[10,1,256]{2,1,0:T(1,128)S(1)} %get-tuple-element.57), channel_id=1, source_target_pairs={{0,1},{1,2},{2,3},{3,4},{4,5},{5,6},{6,7},{8,9},{9,10},{10,11},{11... | collective-permute-start | bytes 30728 | tf_op jit(solution)/shard_map/ppermute | solution.py:20
  167.2 5.9 %collective-permute-start.24 = (f32[1,16,256]{2,1,0:T(8,128)S(1)}, f32[1,16,256]{2,1,0:T(8,128)S(1)}, u32[]{:S(2)}, u32[]{:S(2)}) collective-permute-start(f32[1,16,256]{2,1,0:T(8,128)S(1)} %get-tuple-element.76), channel_id=1, source_target_pairs={{8,0},{16,8},{24,16},{9,1},{17,9},{25,17},{10,2},{18,10},{26,18},{... | collective-permute-start | bytes 49160 | tf_op jit(solution)/shard_map/ppermute | solution.py:23
  169.1 6.5 %collective-permute-start.25 = (f32[1,16,256]{2,1,0:T(8,128)S(1)}, f32[1,16,256]{2,1,0:T(8,128)S(1)}, u32[]{:S(2)}, u32[]{:S(2)}) collective-permute-start(f32[1,16,256]{2,1,0:T(8,128)S(1)} %get-tuple-element.75), channel_id=1, source_target_pairs={{0,8},{8,16},{16,24},{1,9},{9,17},{17,25},{2,10},{10,18},{18,26},{... | collective-permute-start | bytes 49160 | tf_op jit(solution)/shard_map/ppermute | solution.py:20
  175.7 6.1 %collective-permute-start.26 = (f32[10,1,256]{2,1,0:T(1,128)S(1)}, f32[10,1,256]{2,1,0:T(1,128)S(1)}, u32[]{:S(2)}, u32[]{:S(2)}) collective-permute-start(f32[10,1,256]{2,1,0:T(1,128)S(1)} %get-tuple-element.56), channel_id=1, source_target_pairs={{1,0},{2,1},{3,2},{4,3},{5,4},{6,5},{7,6},{9,8},{10,9},{11,10},{12... | collective-permute-start | bytes 30728 | tf_op jit(solution)/shard_map/ppermute | solution.py:23
  183.0 5.9 %collective-permute-start.28 = (f32[1,16,256]{2,1,0:T(8,128)S(1)}, f32[1,16,256]{2,1,0:T(8,128)S(1)}, u32[]{:S(2)}, u32[]{:S(2)}) collective-permute-start(f32[1,16,256]{2,1,0:T(8,128)S(1)} %get-tuple-element.74), channel_id=1, source_target_pairs={{8,0},{16,8},{24,16},{9,1},{17,9},{25,17},{10,2},{18,10},{26,18},{... | collective-permute-start | bytes 49160 | tf_op jit(solution)/shard_map/ppermute | solution.py:23
  184.9 6.5 %collective-permute-start.29 = (f32[1,16,256]{2,1,0:T(8,128)S(1)}, f32[1,16,256]{2,1,0:T(8,128)S(1)}, u32[]{:S(2)}, u32[]{:S(2)}) collective-permute-start(f32[1,16,256]{2,1,0:T(8,128)S(1)} %get-tuple-element.73), channel_id=1, source_target_pairs={{0,8},{8,16},{16,24},{1,9},{9,17},{17,25},{2,10},{10,18},{18,26},{... | collective-permute-start | bytes 49160 | tf_op jit(solution)/shard_map/ppermute | solution.py:20
  191.5 6.1 %collective-permute-start.30 = (f32[10,1,256]{2,1,0:T(1,128)S(1)}, f32[10,1,256]{2,1,0:T(1,128)S(1)}, u32[]{:S(2)}, u32[]{:S(2)}) collective-permute-start(f32[10,1,256]{2,1,0:T(1,128)S(1)} %get-tuple-element.54), channel_id=1, source_target_pairs={{1,0},{2,1},{3,2},{4,3},{5,4},{6,5},{7,6},{9,8},{10,9},{11,10},{12... | collective-permute-start | bytes 30728 | tf_op jit(solution)/shard_map/ppermute | solution.py:23
  198.9 6.0 %collective-permute-start.32 = (f32[3,1,16,256]{3,2,1,0:T(8,128)S(1)}, f32[3,1,16,256]{3,2,1,0:T(8,128)S(1)}, u32[]{:S(2)}, u32[]{:S(2)}) collective-permute-start(f32[3,1,16,256]{3,2,1,0:T(8,128)S(1)} %get-tuple-element.32), channel_id=1, source_target_pairs={{8,0},{16,8},{24,16},{9,1},{17,9},{25,17},{10,2},{18,10},{26,18},{... | collective-permute-start | bytes 147464 | tf_op jit(solution)/shard_map/ppermute | solution.py:23
  200.8 6.9 %collective-permute-start.33 = (f32[3,1,16,256]{3,2,1,0:T(8,128)S(1)}, f32[3,1,16,256]{3,2,1,0:T(8,128)S(1)}, u32[]{:S(2)}, u32[]{:S(2)}) collective-permute-start(f32[3,1,16,256]{3,2,1,0:T(8,128)S(1)} %get-tuple-element.31), channel_id=1, source_target_pairs={{0,8},{8,16},{16,24},{1,9},{9,17},{17,25},{2,10},{10,18},{18,26},{... | collective-permute-start | bytes 147464 | tf_op jit(solution)/shard_map/ppermute | solution.py:20
  207.8 6.1 %collective-permute-start.34 = (f32[3,10,1,256]{3,2,1,0:T(1,128)S(1)}, f32[3,10,1,256]{3,2,1,0:T(1,128)S(1)}, u32[]{:S(2)}, u32[]{:S(2)}) collective-permute-start(f32[3,10,1,256]{3,2,1,0:T(1,128)S(1)} %get-tuple-element.24), channel_id=1, source_target_pairs={{1,0},{2,1},{3,2},{4,3},{5,4},{6,5},{7,6},{9,8},{10,9},{11,10},{12... | collective-permute-start | bytes 92168 | tf_op jit(solution)/shard_map/ppermute | solution.py:23
  215.9 6.0 %collective-permute-start.36 = (f32[3,1,16,256]{3,2,1,0:T(8,128)S(1)}, f32[3,1,16,256]{3,2,1,0:T(8,128)S(1)}, u32[]{:S(2)}, u32[]{:S(2)}) collective-permute-start(f32[3,1,16,256]{3,2,1,0:T(8,128)S(1)} %get-tuple-element.30), channel_id=1, source_target_pairs={{8,0},{16,8},{24,16},{9,1},{17,9},{25,17},{10,2},{18,10},{26,18},{... | collective-permute-start | bytes 147464 | tf_op jit(solution)/shard_map/ppermute | solution.py:23
  217.8 6.9 %collective-permute-start.37 = (f32[3,1,16,256]{3,2,1,0:T(8,128)S(1)}, f32[3,1,16,256]{3,2,1,0:T(8,128)S(1)}, u32[]{:S(2)}, u32[]{:S(2)}) collective-permute-start(f32[3,1,16,256]{3,2,1,0:T(8,128)S(1)} %get-tuple-element.29), channel_id=1, source_target_pairs={{0,8},{8,16},{16,24},{1,9},{9,17},{17,25},{2,10},{10,18},{18,26},{... | collective-permute-start | bytes 147464 | tf_op jit(solution)/shard_map/ppermute | solution.py:20
  224.8 6.3 %collective-permute-start.38 = (f32[3,10,1,256]{3,2,1,0:T(1,128)S(1)}, f32[3,10,1,256]{3,2,1,0:T(1,128)S(1)}, u32[]{:S(2)}, u32[]{:S(2)}) collective-permute-start(f32[3,10,1,256]{3,2,1,0:T(1,128)S(1)} %get-tuple-element.22), channel_id=1, source_target_pairs={{1,0},{2,1},{3,2},{4,3},{5,4},{6,5},{7,6},{9,8},{10,9},{11,10},{12... | collective-permute-start | bytes 92168 | tf_op jit(solution)/shard_map/ppermute | solution.py:23
  232.8 5.9 %collective-permute-start.40 = (f32[1,16,256]{2,1,0:T(8,128)S(1)}, f32[1,16,256]{2,1,0:T(8,128)S(1)}, u32[]{:S(2)}, u32[]{:S(2)}) collective-permute-start(f32[1,16,256]{2,1,0:T(8,128)S(1)} %get-tuple-element.72), channel_id=1, source_target_pairs={{8,0},{16,8},{24,16},{9,1},{17,9},{25,17},{10,2},{18,10},{26,18},{... | collective-permute-start | bytes 49160 | tf_op jit(solution)/shard_map/ppermute | solution.py:23
  234.7 6.5 %collective-permute-start.41 = (f32[1,16,256]{2,1,0:T(8,128)S(1)}, f32[1,16,256]{2,1,0:T(8,128)S(1)}, u32[]{:S(2)}, u32[]{:S(2)}) collective-permute-start(f32[1,16,256]{2,1,0:T(8,128)S(1)} %get-tuple-element.71), channel_id=1, source_target_pairs={{0,8},{8,16},{16,24},{1,9},{9,17},{17,25},{2,10},{10,18},{18,26},{... | collective-permute-start | bytes 49160 | tf_op jit(solution)/shard_map/ppermute | solution.py:20
  241.3 6.3 %collective-permute-start.42 = (f32[10,1,256]{2,1,0:T(1,128)S(1)}, f32[10,1,256]{2,1,0:T(1,128)S(1)}, u32[]{:S(2)}, u32[]{:S(2)}) collective-permute-start(f32[10,1,256]{2,1,0:T(1,128)S(1)} %get-tuple-element.50), channel_id=1, source_target_pairs={{1,0},{2,1},{3,2},{4,3},{5,4},{6,5},{7,6},{9,8},{10,9},{11,10},{12... | collective-permute-start | bytes 30728 | tf_op jit(solution)/shard_map/ppermute | solution.py:23
  242.6 5.8 %collective-permute-start.43 = (f32[10,1,256]{2,1,0:T(1,128)S(1)}, f32[10,1,256]{2,1,0:T(1,128)S(1)}, u32[]{:S(2)}, u32[]{:S(2)}) collective-permute-start(f32[10,1,256]{2,1,0:T(1,128)S(1)} %get-tuple-element.49), channel_id=1, source_target_pairs={{0,1},{1,2},{2,3},{3,4},{4,5},{5,6},{6,7},{8,9},{9,10},{10,11},{11... | collective-permute-start | bytes 30728 | tf_op jit(solution)/shard_map/ppermute | solution.py:20
  248.8 5.9 %collective-permute-start.44 = (f32[1,16,256]{2,1,0:T(8,128)S(1)}, f32[1,16,256]{2,1,0:T(8,128)S(1)}, u32[]{:S(2)}, u32[]{:S(2)}) collective-permute-start(f32[1,16,256]{2,1,0:T(8,128)S(1)} %get-tuple-element.70), channel_id=1, source_target_pairs={{8,0},{16,8},{24,16},{9,1},{17,9},{25,17},{10,2},{18,10},{26,18},{... | collective-permute-start | bytes 49160 | tf_op jit(solution)/shard_map/ppermute | solution.py:23
  250.7 6.5 %collective-permute-start.45 = (f32[1,16,256]{2,1,0:T(8,128)S(1)}, f32[1,16,256]{2,1,0:T(8,128)S(1)}, u32[]{:S(2)}, u32[]{:S(2)}) collective-permute-start(f32[1,16,256]{2,1,0:T(8,128)S(1)} %get-tuple-element.69), channel_id=1, source_target_pairs={{0,8},{8,16},{16,24},{1,9},{9,17},{17,25},{2,10},{10,18},{18,26},{... | collective-permute-start | bytes 49160 | tf_op jit(solution)/shard_map/ppermute | solution.py:20
  257.3 6.1 %collective-permute-start.46 = (f32[10,1,256]{2,1,0:T(1,128)S(1)}, f32[10,1,256]{2,1,0:T(1,128)S(1)}, u32[]{:S(2)}, u32[]{:S(2)}) collective-permute-start(f32[10,1,256]{2,1,0:T(1,128)S(1)} %get-tuple-element.48), channel_id=1, source_target_pairs={{1,0},{2,1},{3,2},{4,3},{5,4},{6,5},{7,6},{9,8},{10,9},{11,10},{12... | collective-permute-start | bytes 30728 | tf_op jit(solution)/shard_map/ppermute | solution.py:23
  264.7 5.9 %collective-permute-start.48 = (f32[1,16,256]{2,1,0:T(8,128)S(1)}, f32[1,16,256]{2,1,0:T(8,128)S(1)}, u32[]{:S(2)}, u32[]{:S(2)}) collective-permute-start(f32[1,16,256]{2,1,0:T(8,128)S(1)} %get-tuple-element.68), channel_id=1, source_target_pairs={{8,0},{16,8},{24,16},{9,1},{17,9},{25,17},{10,2},{18,10},{26,18},{... | collective-permute-start | bytes 49160 | tf_op jit(solution)/shard_map/ppermute | solution.py:23
  266.6 6.5 %collective-permute-start.49 = (f32[1,16,256]{2,1,0:T(8,128)S(1)}, f32[1,16,256]{2,1,0:T(8,128)S(1)}, u32[]{:S(2)}, u32[]{:S(2)}) collective-permute-start(f32[1,16,256]{2,1,0:T(8,128)S(1)} %get-tuple-element.67), channel_id=1, source_target_pairs={{0,8},{8,16},{16,24},{1,9},{9,17},{17,25},{2,10},{10,18},{18,26},{... | collective-permute-start | bytes 49160 | tf_op jit(solution)/shard_map/ppermute | solution.py:20
  273.2 6.1 %collective-permute-start.50 = (f32[10,1,256]{2,1,0:T(1,128)S(1)}, f32[10,1,256]{2,1,0:T(1,128)S(1)}, u32[]{:S(2)}, u32[]{:S(2)}) collective-permute-start(f32[10,1,256]{2,1,0:T(1,128)S(1)} %get-tuple-element.46), channel_id=1, source_target_pairs={{1,0},{2,1},{3,2},{4,3},{5,4},{6,5},{7,6},{9,8},{10,9},{11,10},{12... | collective-permute-start | bytes 30728 | tf_op jit(solution)/shard_map/ppermute | solution.py:23
  280.5 5.9 %collective-permute-start.52 = (f32[1,16,256]{2,1,0:T(8,128)S(1)}, f32[1,16,256]{2,1,0:T(8,128)S(1)}, u32[]{:S(2)}, u32[]{:S(2)}) collective-permute-start(f32[1,16,256]{2,1,0:T(8,128)S(1)} %get-tuple-element.66), channel_id=1, source_target_pairs={{8,0},{16,8},{24,16},{9,1},{17,9},{25,17},{10,2},{18,10},{26,18},{... | collective-permute-start | bytes 49160 | tf_op jit(solution)/shard_map/ppermute | solution.py:23
  282.4 6.5 %collective-permute-start.53 = (f32[1,16,256]{2,1,0:T(8,128)S(1)}, f32[1,16,256]{2,1,0:T(8,128)S(1)}, u32[]{:S(2)}, u32[]{:S(2)}) collective-permute-start(f32[1,16,256]{2,1,0:T(8,128)S(1)} %get-tuple-element.65), channel_id=1, source_target_pairs={{0,8},{8,16},{16,24},{1,9},{9,17},{17,25},{2,10},{10,18},{18,26},{... | collective-permute-start | bytes 49160 | tf_op jit(solution)/shard_map/ppermute | solution.py:20
  289.0 29.2 %collective-permute-start.54 = (f32[10,1,256]{2,1,0:T(1,128)S(1)}, f32[10,1,256]{2,1,0:T(1,128)S(1)}, u32[]{:S(2)}, u32[]{:S(2)}) collective-permute-start(f32[10,1,256]{2,1,0:T(1,128)S(1)} %get-tuple-element.44), channel_id=1, source_target_pairs={{1,0},{2,1},{3,2},{4,3},{5,4},{6,5},{7,6},{9,8},{10,9},{11,10},{12... | collective-permute-start | bytes 30728 | tf_op jit(solution)/shard_map/ppermute | solution.py:23
  290.3 27.9 %collective-permute-start.55 = (f32[10,1,256]{2,1,0:T(1,128)S(1)}, f32[10,1,256]{2,1,0:T(1,128)S(1)}, u32[]{:S(2)}, u32[]{:S(2)}) collective-permute-start(f32[10,1,256]{2,1,0:T(1,128)S(1)} %get-tuple-element.43), channel_id=1, source_target_pairs={{0,1},{1,2},{2,3},{3,4},{4,5},{5,6},{6,7},{8,9},{9,10},{10,11},{11... | collective-permute-start | bytes 30728 | tf_op jit(solution)/shard_map/ppermute | solution.py:20
  349.4 13.1 %all-to-all-start.2 = ((f32[8,1,1,1,4,512]{5,4,3,2,1,0:T(4,128)}), f32[8,1,1,1,4,512]{5,4,3,2,1,0:T(4,128)S(1)}, u32[]{:S(2)}, u32[]{:S(2)}) async-start(f32[8,1,1,1,4,512]{5,4,3,2,1,0:T(4,128)} %constant_dynamic-update-slice_fusion.6), calls=%async_computation.2 | async-start | bytes 131072 | tf_op jit(solution)/shard_map/all_to_all | solution.py:140
  (35 other events, 372.3 us)
